TPU v7x, 512 devices: a whole 4x4x16 slice. The times are simulated.
512 devices in a mesh: seq: 64 (over x, z), head: 8 (over y, core).
Axes of the slice: x: 4, y: 4, z: 16, core: 2. Of those that a mesh axis runs over, the one named last changes fastest.
Arguments:
- lin_query: bfloat16 [32768, 4096], P('seq', 'head'), may hold values from -6 to 6
- lin_key: bfloat16 [32768, 4096], P('seq', 'head'), may hold values from -6 to 6
- lin_value: bfloat16 [32768, 4096], P('seq', 'head'), may hold values from -54 to 54
- lin_gate: bfloat16 [32768, 4096], P('seq', 'head'), may hold values from -6 to 6
- log_decay: float32 [32768, 32], P('seq', 'head'), as said below
- norm_gain: float32 [4096], P('head'), may hold values from 0.1 to 1.9
- soft_query: bfloat16 [32768, 4096], P('seq', 'head'), may hold values from -4.5 to 4.5
- soft_key: bfloat16 [32768, 1024], P('seq', 'head'), may hold values from -4.5 to 4.5
- soft_value: bfloat16 [32768, 1024], P('seq', 'head'), may hold values from -6 to 6
- doc_ids: int32 [256], replicated, may hold values from 0 to 31, never falling along the last dimension, each value on 1 to 29 neighbouring positions
Outputs:
- lin_out: bfloat16 [32768, 4096], P('seq', 'head')
- soft_out: bfloat16 [32768, 4096], P('seq', 'head')
Inputs may be any that keep to these rules, and one draw needn't show every extreme that they name: `log_decay`: every entry is below zero. `doc_ids`: never falling along the window; every document covers 1 to 29 mask blocks, one exactly 29.
All inputs are finite; a program needn't handle non-finite values.
Results may differ from a plain program's by a relative error of at most 0.004.
Values may be sent and summed in bfloat16 or wider, within the bound.
No kernel may reach another device: no remote copies, remote signals or barrier semaphores. Data moves between devices by JAX's collectives and lax.ppermute only.
A program may use at most 128 MiB of HBM per device.

v0:
```python
import jax
import jax.numpy as jnp
from jax import lax
from jax.sharding import PartitionSpec as P

HD = 128
BLK = 256
DOC_MOST = 29


eps = 1e-06


def entering_2(array, axis, combine, identity):
    peers, position = (lax.axis_size(axis), lax.axis_index(axis))
    everything = jax.tree.map(lambda part: lax.all_gather(part, axis), array)
    start = jax.tree.map(
        lambda part, zero: jnp.broadcast_to(jnp.asarray(zero, part.dtype), part.shape),
        array,
        identity,
    )

    def turn(k, before):
        reached = k < position
        new = combine(before, jax.tree.map(lambda part: part[k], everything))
        return jax.tree.map(lambda a, b: jnp.where(reached, a, b), new, before)

    return lax.fori_loop(0, peers, turn, start)


def from_behind(value, axis, steps):
    count = lax.axis_size(axis)
    first, last = (max(0, -steps), min(count, count - steps))
    return lax.ppermute(value, axis, [(source, source + steps) for source in range(first, last)])


def chain_combine(earlier, later_pair):
    return (earlier[0] * later_pair[0], later_pair[0][:, None, None] * earlier[1] + later_pair[1])


def lightning(lin_query, lin_key, lin_value, lin_gate, log_decay, norm_gain):
    row_count, features = lin_query.shape
    head_count = log_decay.shape[1]
    block_count = row_count // BLK
    high = lax.Precision.HIGHEST
    query_matrix = lin_query.reshape(block_count, BLK, head_count, HD)
    key_rows = lin_key.reshape(block_count, BLK, head_count, HD)
    values = lin_value.reshape(block_count, BLK, head_count, HD)
    cumulative = jnp.cumsum(log_decay.reshape(block_count, BLK, head_count), axis=1)
    cum_heads = jnp.swapaxes(cumulative, 1, 2)
    causal = lax.broadcasted_iota(jnp.int32, (BLK, BLK), 0) >= lax.broadcasted_iota(
        jnp.int32, (BLK, BLK), 1
    )
    gap_sums = cum_heads[:, :, :, None] - cum_heads[:, :, None, :]
    weight = jnp.exp(jnp.where(causal[None, None], gap_sums, -1e30))
    scores = jnp.einsum(
        "btha,bsha->bhts", query_matrix, key_rows, preferred_element_type=jnp.float32
    )
    mixed_scores = (scores * weight).astype(jnp.bfloat16)
    intra_term = jnp.einsum(
        "bhts,bsha->btha", mixed_scores, values, preferred_element_type=jnp.float32
    )
    block_total = cumulative[:, -1, :]
    factors = jnp.exp(block_total)
    weighted = (
        key_rows.astype(jnp.float32) * jnp.exp(block_total[:, None, :] - cumulative)[..., None]
    )
    local_state = jnp.einsum(
        "bsha,bshc->bhac", weighted, values.astype(jnp.float32), precision=high
    )

    def fold_block(state_pair, block_item):
        factor, block_state = block_item
        return ((state_pair[0] * factor, factor[:, None, None] * state_pair[1] + block_state), None)

    unit_factor = jnp.ones((head_count,), jnp.float32)
    empty_state = jnp.zeros((head_count, HD, HD), jnp.float32)
    (dev_factor, dev_state), _ = lax.scan(
        fold_block, (unit_factor, empty_state), (factors, local_state)
    )
    incoming = entering_2((dev_factor, dev_state), "seq", chain_combine, (unit_factor, empty_state))

    def walk_block(carried, block_item):
        factor, block_state = block_item
        return (factor[:, None, None] * carried + block_state, carried)

    _, entering = lax.scan(walk_block, incoming[1], (factors, local_state))
    scaled_q = query_matrix.astype(jnp.float32) * jnp.exp(cumulative)[..., None]
    inter_term = jnp.einsum("btha,bhac->bthc", scaled_q, entering, precision=high)
    raw_out = (intra_term + inter_term).reshape(row_count, features)
    squares = jnp.sum(raw_out * raw_out, axis=1)
    sq_total = lax.psum(squares, "head")
    norm_scale = lax.rsqrt(sq_total / (features * lax.axis_size("head")) + eps)
    gated = (
        raw_out
        * norm_scale[:, None]
        * norm_gain[None, :]
        * jax.nn.sigmoid(lin_gate.astype(jnp.float32))
    )
    return gated.astype(jnp.bfloat16)


def attend(soft_query, soft_key, soft_value, doc_ids):
    row_count, features = soft_query.shape
    head_count = features // HD
    kv_count = soft_key.shape[1] // HD
    group_size = head_count // kv_count
    seq_count = lax.axis_size("seq")
    own_index = lax.axis_index("seq")
    blocks_dev = doc_ids.shape[0] // seq_count
    doc_rows = row_count // blocks_dev
    cycle_steps = (DOC_MOST + blocks_dev - 2) // blocks_dev
    query_matrix = soft_query.reshape(row_count, kv_count, group_size, HD)
    key_rows = soft_key.reshape(row_count, kv_count, HD)
    value_rows = soft_value.reshape(row_count, kv_count, HD)
    token_docs = jnp.repeat(doc_ids, doc_rows)
    query_pos = own_index * row_count + lax.iota(jnp.int32, row_count)
    query_docs = lax.dynamic_slice_in_dim(token_docs, own_index * row_count, row_count, 0)

    def absorb(carried, key_segment, value_segment, first_pos):
        piece_rows = key_segment.shape[0]
        key_pos = first_pos + lax.iota(jnp.int32, piece_rows)
        key_docs = lax.dynamic_slice_in_dim(token_docs, jnp.maximum(first_pos, 0), piece_rows, 0)
        allowed = (
            (key_pos[None, :] <= query_pos[:, None])
            & (key_docs[None, :] == query_docs[:, None])
            & (key_pos >= 0)[None, :]
        )
        run_max, run_sum, run_acc = carried
        scores = jnp.einsum(
            "lfnq,yfq->fnly", query_matrix, key_segment, preferred_element_type=jnp.float32
        )
        scores = scores.reshape(head_count, row_count, piece_rows) * HD ** (-0.5)
        scores = jnp.where(allowed[None], scores, -1e30)
        new_max = jnp.maximum(run_max, jnp.max(scores, axis=-1))
        shrink = jnp.exp(run_max - new_max)
        probs = jnp.where(allowed[None], jnp.exp(scores - new_max[:, :, None]), 0.0)
        new_sum = run_sum * shrink + jnp.sum(probs, axis=-1)
        probability_rows = probs.astype(jnp.bfloat16).reshape(
            kv_count, group_size, row_count, piece_rows
        )
        added = jnp.einsum(
            "qcvu,uqw->vqcw", probability_rows, value_segment, preferred_element_type=jnp.float32
        )
        added = added.reshape(row_count, head_count, HD)
        new_acc = run_acc * shrink.T[:, :, None] + added
        return (new_max, new_sum, new_acc)

    start_state = (
        jnp.full((head_count, row_count), -1e30, jnp.float32),
        jnp.zeros((head_count, row_count), jnp.float32),
        jnp.zeros((row_count, head_count, HD), jnp.float32),
    )
    carried = absorb(start_state, key_rows, value_rows, own_index * row_count)

    def cycle_step(step_index, loop_state):
        state_now, moving_keys, moving_values = loop_state
        moving_keys, moving_values = from_behind((moving_keys, moving_values), "seq", 1)
        state_now = absorb(
            state_now, moving_keys, moving_values, (own_index - step_index) * row_count
        )
        return (state_now, moving_keys, moving_values)

    carried, _, _ = lax.fori_loop(1, cycle_steps + 1, cycle_step, (carried, key_rows, value_rows))
    run_max, run_sum, run_acc = carried
    final_output = run_acc / run_sum.T[:, :, None]
    return final_output.reshape(row_count, features).astype(jnp.bfloat16)


def on_device(
    lin_query,
    lin_key,
    lin_value,
    lin_gate,
    log_decay,
    norm_gain,
    soft_query,
    soft_key,
    soft_value,
    doc_ids,
):
    lin_out = lightning(lin_query, lin_key, lin_value, lin_gate, log_decay, norm_gain)
    soft_out = attend(soft_query, soft_key, soft_value, doc_ids)
    return (lin_out, soft_out)


def solution(mesh):
    in_specs = (
        P("seq", "head"),
        P("seq", "head"),
        P("seq", "head"),
        P("seq", "head"),
        P("seq", "head"),
        P("head"),
        P("seq", "head"),
        P("seq", "head"),
        P("seq", "head"),
        P(),
    )
    out_specs = (P("seq", "head"), P("seq", "head"))
    return jax.shard_map(
        on_device, mesh=mesh, in_specs=in_specs, out_specs=out_specs, check_vma=False
    )
```

profile of v0, /device:TPU:7, one launch (start us, length us, event | category | flops | bytes accessed | tf_op | source)
XLA Modules:
  0.0 427.1 jit_solution(16689769506449516520)
XLA Ops:
  10.4 2.4 reduce-window.6
  20.7 101.6 %all-reduce = f32[256]{0:T(256)S(1)} all-reduce(f32[256]{0:T(256)S(1)} %dynamic-update-slice), channel_id=2, replica_groups=mesh['seq'=64,'head'=8] {'seq'}, use_global_device_ids=true, to_apply=%add | all-reduce | flops 256 | bytes 2048
  127.7 2.5 fusion.43
  130.2 125.3 %while.62 = (s32[]{:T(128)}, f32[4,512]{1,0:T(4,128)S(1)}, f32[4,512]{1,0:T(4,128)S(1)}, f32[512,4,128]{2,0,1:T(8,128)}, bf16[512,1,128]{2,0,1:T(8,128)(2,1)S(1)...) while((s32[]{:T(128)}, f32[4,512]{1,0:T(4,128)S(1)}, ...), condition=%wide.region_15.16_spmd.clone, body=%wide.region_12.15_spmd.clone.sunk | while | flops 552083456 | bytes 26625344 | solution.py:164
  134.5 4.3 %collective-permute-done = bf16[512,1,128]{2,0,1:T(8,128)(2,1)S(1)} collective-permute-done((bf16[512,1,128]{2,0,1:T(8,128)(2,1)S(1)}, bf16[512,1,128]{2,0,1:T(8,128)(2,1)S(1)}, u32[]{:S(2)}, u32[]{:S(2)}) %collective-permute-start) | collective-permute-done | bytes 131104 | tf_op jit(solution)/shard_map/while/body/eval_jaxpr/ppermute | solution.py:34
  145.4 4.5 %collective-permute-start.1 = (bf16[512,1,128]{2,0,1:T(8,128)(2,1)S(1)}, bf16[512,1,128]{2,0,1:T(8,128)(2,1)S(1)}, u32[]{:S(2)}, u32[]{:S(2)}) collective-permute-start(bf16[512,1,128]{2,0,1:T(8,128)(2,1)S(1)} %get-tuple-element.772), channel_id=1, source_target_pairs={{0,8},{8,16},{16,24},{24,32},{32,40},{40,48},{48,56},{56,64},{64,7... | collective-permute-start | bytes 393224 | tf_op jit(solution)/shard_map/while/body/eval_jaxpr/ppermute | solution.py:34
  150.3 3.8 collective-permute-done
  156.1 2.2 collective-permute-done.1
  162.9 3.5 collective-permute-start.1
  166.8 6.5 %collective-permute-done = bf16[512,1,128]{2,0,1:T(8,128)(2,1)S(1)} collective-permute-done((bf16[512,1,128]{2,0,1:T(8,128)(2,1)S(1)}, bf16[512,1,128]{2,0,1:T(8,128)(2,1)S(1)}, u32[]{:S(2)}, u32[]{:S(2)}) %collective-permute-start) | collective-permute-done | bytes 131104 | tf_op jit(solution)/shard_map/while/body/eval_jaxpr/ppermute | solution.py:34
  175.3 2.7 collective-permute-done.1
  184.9 8.0 %collective-permute-done = bf16[512,1,128]{2,0,1:T(8,128)(2,1)S(1)} collective-permute-done((bf16[512,1,128]{2,0,1:T(8,128)(2,1)S(1)}, bf16[512,1,128]{2,0,1:T(8,128)(2,1)S(1)}, u32[]{:S(2)}, u32[]{:S(2)}) %collective-permute-start) | collective-permute-done | bytes 131104 | tf_op jit(solution)/shard_map/while/body/eval_jaxpr/ppermute | solution.py:34
  194.9 3.1 collective-permute-done.1
  202.6 1.9 collective-permute-start.1
  205.0 7.9 %collective-permute-done = bf16[512,1,128]{2,0,1:T(8,128)(2,1)S(1)} collective-permute-done((bf16[512,1,128]{2,0,1:T(8,128)(2,1)S(1)}, bf16[512,1,128]{2,0,1:T(8,128)(2,1)S(1)}, u32[]{:S(2)}, u32[]{:S(2)}) %collective-permute-start) | collective-permute-done | bytes 131104 | tf_op jit(solution)/shard_map/while/body/eval_jaxpr/ppermute | solution.py:34
  214.9 3.6 collective-permute-done.1
  225.4 7.6 %collective-permute-done = bf16[512,1,128]{2,0,1:T(8,128)(2,1)S(1)} collective-permute-done((bf16[512,1,128]{2,0,1:T(8,128)(2,1)S(1)}, bf16[512,1,128]{2,0,1:T(8,128)(2,1)S(1)}, u32[]{:S(2)}, u32[]{:S(2)}) %collective-permute-start) | collective-permute-done | bytes 131104 | tf_op jit(solution)/shard_map/while/body/eval_jaxpr/ppermute | solution.py:34
  235.1 3.6 collective-permute-done.1
  245.6 3.5 collective-permute-done
  255.4 2.4 copy_bitcast_fusion
  257.8 112.2 %while.64 = (s32[]{:T(128)}, f32[4,128,128]{2,1,0:T(8,128)S(1)}, s32[]{:T(128)}, f32[64,4]{1,0:T(8,128)}, f32[64,4,128,128]{3,2,1,0:T(8,128)}, /*index=5*/s32[]{:T(128)}, s32[]{:T(128)}) while((s32[]{:T(128)}, f32[4,128,128]{2,1,0:T(8,128)S(1)}, s32[]{:T(128)}, f32[64,4]{1,0:T(8,128)}, f32[64,4,128,128]{3,2,1,0:T(8,128)}, ...), condition=%wide.region_5.6_spmd.clone, body=%wide.region_4.5_spmd.clone.sunk | while | flops 262148 | bytes 786593 | solution.py:28
  371.8 2.4 convolution_bitcast_fusion
  374.3 2.0 multiply_reduce_fusion
  377.8 41.3 %psum.7 = f32[512]{0:T(512)S(1)} all-reduce(f32[512]{0:T(512)S(1)} %bitcast.220), channel_id=1, replica_groups=mesh['seq'=64,'head'=8] {'head'}, use_global_device_ids=true, to_apply=%region_9.10 | all-reduce | flops 512 | bytes 4096 | tf_op jit(solution)/shard_map/psum | solution.py:92
  (332 shorter events, 190.9 us)
Async XLA Ops:
  7.2 117.4 %copy-start = (s32[256]{0:T(256)S(1)}, s32[256]{0:T(256)}, u32[]{:S(2)}) copy-start(s32[256]{0:T(256)} %param.27) | copy-start | bytes 3076
  7.2 250.6 %all-gather.4.cloned.1.call-start = ((), (), s32[]{:S(2)}) async-start(), calls=%async_computation | async-start | bytes 17039360 | tf_op jit(solution)/shard_map/all_gather | solution.py:16
  15.3 107.8 %copy-start.6 = (bf16[512,512]{1,0:T(8,128)(2,1)S(1)}, bf16[512,512]{1,0:T(8,128)(2,1)}, u32[]{:S(2)}) copy-start(bf16[512,512]{1,0:T(8,128)(2,1)} %param.18) | copy-start | bytes 1572868
  15.6 108.5 %copy-start.2 = (bf16[512,512]{1,0:T(8,128)(2,1)S(1)}, bf16[512,512]{1,0:T(8,128)(2,1)}, u32[]{:S(2)}) copy-start(bf16[512,512]{1,0:T(8,128)(2,1)} %param.24) | copy-start | bytes 1572868
  130.2 8.6 %collective-permute-start = (bf16[512,1,128]{2,0,1:T(8,128)(2,1)S(1)}, bf16[512,1,128]{2,0,1:T(8,128)(2,1)S(1)}, u32[]{:S(2)}, u32[]{:S(2)}) collective-permute-start(bf16[512,1,128]{2,0,1:T(8,128)(2,1)S(1)} %get-tuple-element.771), channel_id=1, source_target_pairs={{0,8},{8,16},{16,24},{24,32},{32,40},{40,48},{48,56},{56,64},{64,7... | collective-permute-start | bytes 393224 | tf_op jit(solution)/shard_map/while/body/eval_jaxpr/ppermute | solution.py:34
  132.1 8.7 %collective-permute-start.1 = (bf16[512,1,128]{2,0,1:T(8,128)(2,1)S(1)}, bf16[512,1,128]{2,0,1:T(8,128)(2,1)S(1)}, u32[]{:S(2)}, u32[]{:S(2)}) collective-permute-start(bf16[512,1,128]{2,0,1:T(8,128)(2,1)S(1)} %get-tuple-element.772), channel_id=1, source_target_pairs={{0,8},{8,16},{16,24},{24,32},{32,40},{40,48},{48,56},{56,64},{64,7... | collective-permute-start | bytes 393224 | tf_op jit(solution)/shard_map/while/body/eval_jaxpr/ppermute | solution.py:34
  143.5 10.6 %collective-permute-start = (bf16[512,1,128]{2,0,1:T(8,128)(2,1)S(1)}, bf16[512,1,128]{2,0,1:T(8,128)(2,1)S(1)}, u32[]{:S(2)}, u32[]{:S(2)}) collective-permute-start(bf16[512,1,128]{2,0,1:T(8,128)(2,1)S(1)} %get-tuple-element.771), channel_id=1, source_target_pairs={{0,8},{8,16},{16,24},{24,32},{32,40},{40,48},{48,56},{56,64},{64,7... | collective-permute-start | bytes 393224 | tf_op jit(solution)/shard_map/while/body/eval_jaxpr/ppermute | solution.py:34
  145.4 12.9 %collective-permute-start.1 = (bf16[512,1,128]{2,0,1:T(8,128)(2,1)S(1)}, bf16[512,1,128]{2,0,1:T(8,128)(2,1)S(1)}, u32[]{:S(2)}, u32[]{:S(2)}) collective-permute-start(bf16[512,1,128]{2,0,1:T(8,128)(2,1)S(1)} %get-tuple-element.772), channel_id=1, source_target_pairs={{0,8},{8,16},{16,24},{24,32},{32,40},{40,48},{48,56},{56,64},{64,7... | collective-permute-start | bytes 393224 | tf_op jit(solution)/shard_map/while/body/eval_jaxpr/ppermute | solution.py:34
  161.0 12.3 %collective-permute-start = (bf16[512,1,128]{2,0,1:T(8,128)(2,1)S(1)}, bf16[512,1,128]{2,0,1:T(8,128)(2,1)S(1)}, u32[]{:S(2)}, u32[]{:S(2)}) collective-permute-start(bf16[512,1,128]{2,0,1:T(8,128)(2,1)S(1)} %get-tuple-element.771), channel_id=1, source_target_pairs={{0,8},{8,16},{16,24},{24,32},{32,40},{40,48},{48,56},{56,64},{64,7... | collective-permute-start | bytes 393224 | tf_op jit(solution)/shard_map/while/body/eval_jaxpr/ppermute | solution.py:34
  162.9 15.1 %collective-permute-start.1 = (bf16[512,1,128]{2,0,1:T(8,128)(2,1)S(1)}, bf16[512,1,128]{2,0,1:T(8,128)(2,1)S(1)}, u32[]{:S(2)}, u32[]{:S(2)}) collective-permute-start(bf16[512,1,128]{2,0,1:T(8,128)(2,1)S(1)} %get-tuple-element.772), channel_id=1, source_target_pairs={{0,8},{8,16},{16,24},{24,32},{32,40},{40,48},{48,56},{56,64},{64,7... | collective-permute-start | bytes 393224 | tf_op jit(solution)/shard_map/while/body/eval_jaxpr/ppermute | solution.py:34
  173.3 4.7 %copy-start.4 = (f32[512,4,128]{2,0,1:T(8,128)S(1)}, f32[512,4,128]{2,0,1:T(8,128)}, u32[]{:S(2)}) copy-start(f32[512,4,128]{2,0,1:T(8,128)} %get-tuple-element.770) | copy-start | bytes 3145732 | tf_op jit(solution)/shard_map/while
  180.7 12.3 %collective-permute-start = (bf16[512,1,128]{2,0,1:T(8,128)(2,1)S(1)}, bf16[512,1,128]{2,0,1:T(8,128)(2,1)S(1)}, u32[]{:S(2)}, u32[]{:S(2)}) collective-permute-start(bf16[512,1,128]{2,0,1:T(8,128)(2,1)S(1)} %get-tuple-element.771), channel_id=1, source_target_pairs={{0,8},{8,16},{16,24},{24,32},{32,40},{40,48},{48,56},{56,64},{64,7... | collective-permute-start | bytes 393224 | tf_op jit(solution)/shard_map/while/body/eval_jaxpr/ppermute | solution.py:34
  182.6 15.5 %collective-permute-start.1 = (bf16[512,1,128]{2,0,1:T(8,128)(2,1)S(1)}, bf16[512,1,128]{2,0,1:T(8,128)(2,1)S(1)}, u32[]{:S(2)}, u32[]{:S(2)}) collective-permute-start(bf16[512,1,128]{2,0,1:T(8,128)(2,1)S(1)} %get-tuple-element.772), channel_id=1, source_target_pairs={{0,8},{8,16},{16,24},{24,32},{32,40},{40,48},{48,56},{56,64},{64,7... | collective-permute-start | bytes 393224 | tf_op jit(solution)/shard_map/while/body/eval_jaxpr/ppermute | solution.py:34
  192.9 5.1 %copy-start.4 = (f32[512,4,128]{2,0,1:T(8,128)S(1)}, f32[512,4,128]{2,0,1:T(8,128)}, u32[]{:S(2)}) copy-start(f32[512,4,128]{2,0,1:T(8,128)} %get-tuple-element.770) | copy-start | bytes 3145732 | tf_op jit(solution)/shard_map/while
  200.7 12.2 %collective-permute-start = (bf16[512,1,128]{2,0,1:T(8,128)(2,1)S(1)}, bf16[512,1,128]{2,0,1:T(8,128)(2,1)S(1)}, u32[]{:S(2)}, u32[]{:S(2)}) collective-permute-start(bf16[512,1,128]{2,0,1:T(8,128)(2,1)S(1)} %get-tuple-element.771), channel_id=1, source_target_pairs={{0,8},{8,16},{16,24},{24,32},{32,40},{40,48},{48,56},{56,64},{64,7... | collective-permute-start | bytes 393224 | tf_op jit(solution)/shard_map/while/body/eval_jaxpr/ppermute | solution.py:34
  202.6 15.9 %collective-permute-start.1 = (bf16[512,1,128]{2,0,1:T(8,128)(2,1)S(1)}, bf16[512,1,128]{2,0,1:T(8,128)(2,1)S(1)}, u32[]{:S(2)}, u32[]{:S(2)}) collective-permute-start(bf16[512,1,128]{2,0,1:T(8,128)(2,1)S(1)} %get-tuple-element.772), channel_id=1, source_target_pairs={{0,8},{8,16},{16,24},{24,32},{32,40},{40,48},{48,56},{56,64},{64,7... | collective-permute-start | bytes 393224 | tf_op jit(solution)/shard_map/while/body/eval_jaxpr/ppermute | solution.py:34
  212.9 5.6 %copy-start.4 = (f32[512,4,128]{2,0,1:T(8,128)S(1)}, f32[512,4,128]{2,0,1:T(8,128)}, u32[]{:S(2)}) copy-start(f32[512,4,128]{2,0,1:T(8,128)} %get-tuple-element.770) | copy-start | bytes 3145732 | tf_op jit(solution)/shard_map/while
  221.2 11.9 %collective-permute-start = (bf16[512,1,128]{2,0,1:T(8,128)(2,1)S(1)}, bf16[512,1,128]{2,0,1:T(8,128)(2,1)S(1)}, u32[]{:S(2)}, u32[]{:S(2)}) collective-permute-start(bf16[512,1,128]{2,0,1:T(8,128)(2,1)S(1)} %get-tuple-element.771), channel_id=1, source_target_pairs={{0,8},{8,16},{16,24},{24,32},{32,40},{40,48},{48,56},{56,64},{64,7... | collective-permute-start | bytes 393224 | tf_op jit(solution)/shard_map/while/body/eval_jaxpr/ppermute | solution.py:34
  223.1 15.6 %collective-permute-start.1 = (bf16[512,1,128]{2,0,1:T(8,128)(2,1)S(1)}, bf16[512,1,128]{2,0,1:T(8,128)(2,1)S(1)}, u32[]{:S(2)}, u32[]{:S(2)}) collective-permute-start(bf16[512,1,128]{2,0,1:T(8,128)(2,1)S(1)} %get-tuple-element.772), channel_id=1, source_target_pairs={{0,8},{8,16},{16,24},{24,32},{32,40},{40,48},{48,56},{56,64},{64,7... | collective-permute-start | bytes 393224 | tf_op jit(solution)/shard_map/while/body/eval_jaxpr/ppermute | solution.py:34
  233.1 5.6 %copy-start.4 = (f32[512,4,128]{2,0,1:T(8,128)S(1)}, f32[512,4,128]{2,0,1:T(8,128)}, u32[]{:S(2)}) copy-start(f32[512,4,128]{2,0,1:T(8,128)} %get-tuple-element.770) | copy-start | bytes 3145732 | tf_op jit(solution)/shard_map/while
  241.3 7.8 %collective-permute-start = (bf16[512,1,128]{2,0,1:T(8,128)(2,1)S(1)}, bf16[512,1,128]{2,0,1:T(8,128)(2,1)S(1)}, u32[]{:S(2)}, u32[]{:S(2)}) collective-permute-start(bf16[512,1,128]{2,0,1:T(8,128)(2,1)S(1)} %get-tuple-element.771), channel_id=1, source_target_pairs={{0,8},{8,16},{16,24},{24,32},{32,40},{40,48},{48,56},{56,64},{64,7... | collective-permute-start | bytes 393224 | tf_op jit(solution)/shard_map/while/body/eval_jaxpr/ppermute | solution.py:34
  243.3 9.5 %collective-permute-start.1 = (bf16[512,1,128]{2,0,1:T(8,128)(2,1)S(1)}, bf16[512,1,128]{2,0,1:T(8,128)(2,1)S(1)}, u32[]{:S(2)}, u32[]{:S(2)}) collective-permute-start(bf16[512,1,128]{2,0,1:T(8,128)(2,1)S(1)} %get-tuple-element.772), channel_id=1, source_target_pairs={{0,8},{8,16},{16,24},{24,32},{32,40},{40,48},{48,56},{56,64},{64,7... | collective-permute-start | bytes 393224 | tf_op jit(solution)/shard_map/while/body/eval_jaxpr/ppermute | solution.py:34
  374.2 44.9 %copy-start.7 = (bf16[512,512]{1,0:T(8,128)(2,1)S(1)}, bf16[512,512]{1,0:T(8,128)(2,1)}, u32[]{:S(2)}) copy-start(bf16[512,512]{1,0:T(8,128)(2,1)} %param.21) | copy-start | bytes 1572868
  374.2 44.9 %copy-start.11 = (f32[512]{0:T(512)S(1)}, f32[512]{0:T(512)}, u32[]{:S(2)}) copy-start(f32[512]{0:T(512)} %param.23) | copy-start | bytes 6148
  (15 other events, 27.3 us)
Sparse Core Ops, SparseCore 0:
  18.7 218.2 all-gather.3
where the time goes:
time: 432 us; the launch traced here: 427 us
  blocking collectives  143 us (33%)
  other arithmetic  86.1 us (20%)
  local copies, waits for them, and re-layouts  65.6 us (15%)
  waiting for transfers between devices  58.5 us (14%)
  starting transfers between devices  31 us (7%)
  matrix products  26.1 us (6%)
  between operations  14.9 us (3%)
    unnamed x1, blocking collectives  102 us
    select_n x64, other arithmetic, turn(): return jax.tree.map(lambda a, b: jnp.where(reached, a, b), new, before)  67.1 us
    ppermute x14, waiting for transfers between devices, from_behind(): lax.ppermute(value, axis, [(source, source + steps) for source in range(f...  58.5 us
    mul x64, local copies, waits for them, and re-layouts, chain_combine(): later_pair[0][:, None, None] * earlier[1] + later_pair[1]  44 us
    psum x1, blocking collectives, lightning(): sq_total = lax.psum(squares, 'head')  41.3 us
    ppermute x14, starting transfers between devices, from_behind(): lax.ppermute(value, axis, [(source, source + steps) for source in range(f...  30.9 us
    dot_general x8, matrix products, absorb(): jnp.einsum('qcvu,uqw->vqcw', probability_rows, value_segment, preferred_e...  14 us
  transfers between devices with their start and end apart: 15, of which 13 were waited for; matrix products, arithmetic and copies ran while one was open for 9% of the time, Pallas kernels for 0%

commit v1 on v0

v1 whole, which is shorter than its diff:
```python
import functools
import math

import jax
import jax.numpy as jnp
import numpy as np
from jax import lax
from jax.experimental import pallas as pl
from jax.experimental.pallas import tpu as pltpu
from jax.sharding import PartitionSpec as P

HD = 128
BLK = 256
MBLK = 128
DOC_MOST = 29
EPS = 1e-06
NEG = -1e30
LOG_FLOOR = -1000.0
LOG_ROWS = 16
QUAD = 4
F32 = jnp.float32
BF16 = jnp.bfloat16
VMEM_LIMIT = 48 * 1024 * 1024


def call(body, outs, operands, *, flops, moved, exps=0, scratch=(), smem=(), aliases=None):
    specs = [
        pl.BlockSpec(memory_space=pltpu.SMEM if i in smem else pltpu.VMEM)
        for i in range(len(operands))
    ]
    return pl.pallas_call(
        body,
        out_shape=outs,
        in_specs=specs,
        out_specs=jax.tree.map(lambda _: pl.BlockSpec(memory_space=pltpu.VMEM), outs),
        scratch_shapes=list(scratch),
        input_output_aliases=aliases or {},
        compiler_params=pltpu.CompilerParams(vmem_limit_bytes=VMEM_LIMIT),
        cost_estimate=pl.CostEstimate(
            flops=int(flops), bytes_accessed=int(moved), transcendentals=int(exps)
        ),
    )(*operands)


def dot(a, b, dims, precision=None):
    return lax.dot_general(
        a, b, (dims, ((), ())), preferred_element_type=F32, precision=precision
    )


def split(x):
    high = x.astype(BF16)
    return high, (x - high.astype(F32)).astype(BF16)


def block_sums(log_ref):
    rows = lax.broadcasted_iota(jnp.int32, (BLK, BLK), 0)
    cols = lax.broadcasted_iota(jnp.int32, (BLK, BLK), 1)
    tri = (rows >= cols).astype(F32)
    return [
        dot(tri, log_ref[b * BLK : (b + 1) * BLK, :], ((1,), (0,)), lax.Precision.HIGHEST)
        for b in range(log_ref.shape[0] // BLK)
    ]


def log_rows(total):
    first = total.astype(BF16).astype(F32)
    second = (total - first).astype(BF16).astype(F32)
    third = total - first - second
    row = lax.broadcasted_iota(jnp.int32, (LOG_ROWS, HD), 0)
    packed = jnp.where(row == 0, first, jnp.where(row == 1, second, jnp.where(row == 2, third, 0.0)))
    return packed.astype(BF16)


def states_body(key_ref, value_ref, log_ref, send_ref, first_ref):
    heads = key_ref.shape[1] // HD
    sums = block_sums(log_ref)
    ends = [s[BLK - 1 : BLK, :] for s in sums]
    for h in range(heads):
        lanes = slice(h * HD, (h + 1) * HD)
        state = None
        total = jnp.zeros((1, 1), F32)
        for b, cum in enumerate(sums):
            rows = slice(b * BLK, (b + 1) * BLK)
            end = ends[b][:, h : h + 1]
            weight = jnp.exp(end - cum[:, h : h + 1])
            high, low = split(key_ref[rows, lanes].astype(F32) * weight)
            value = value_ref[rows, lanes]
            local = dot(high, value, ((0,), (0,))) + dot(low, value, ((0,), (0,)))
            if b == 0:
                first_ref[h] = local
                state = local
            else:
                state = jnp.exp(end) * state + local
            total = total + end
        send_ref[h, :HD, :] = state.astype(BF16)
        total = jnp.broadcast_to(jnp.maximum(total, LOG_FLOOR), (1, HD))
        send_ref[h, HD:, :] = log_rows(total)


def local_body(query_ref, key_ref, value_ref, log_ref, first_ref, raw_ref):
    heads = key_ref.shape[1] // HD
    sums = block_sums(log_ref)
    across = [s.T for s in sums]
    rows_i = lax.broadcasted_iota(jnp.int32, (BLK, BLK), 0)
    cols_i = lax.broadcasted_iota(jnp.int32, (BLK, BLK), 1)
    causal = rows_i >= cols_i
    for b, cum in enumerate(sums):
        rows = slice(b * BLK, (b + 1) * BLK)
        for h in range(heads):
            lanes = slice(h * HD, (h + 1) * HD)
            column = cum[:, h : h + 1]
            query = query_ref[rows, lanes]
            gap = column - across[b][h : h + 1, :]
            weight = jnp.exp(jnp.where(causal, gap, NEG))
            scores = dot(query, key_ref[rows, lanes], ((1,), (1,)))
            mixed = (scores * weight).astype(BF16)
            raw = dot(mixed, value_ref[rows, lanes], ((1,), (0,)))
            if b > 0:
                high, low = split(first_ref[h])
                inter = dot(query, high, ((1,), (0,))) + dot(query, low, ((1,), (0,)))
                raw = raw + jnp.exp(column) * inter
            raw_ref[rows, lanes] = raw


def log_of(block):
    return jnp.sum(block[HD:, :].astype(F32), axis=0, keepdims=True)


def fold(parts):
    state, total = parts[0]
    for s, l in parts[1:]:
        state = jnp.exp(l) * state + s
        total = total + l
    return state, jnp.maximum(total, LOG_FLOOR)


def parts_of(got_ref):
    return [
        (got_ref[j, :HD, :].astype(F32), log_of(got_ref[j])) for j in range(got_ref.shape[0])
    ]


def group_body(got_ref, send_ref):
    state, total = fold(parts_of(got_ref))
    state = state.astype(BF16)
    rows = log_rows(total)
    for j in range(send_ref.shape[0]):
        send_ref[j, :HD, :] = state
        send_ref[j, HD:, :] = rows


def before(parts, place):
    state = jnp.zeros((HD, HD), F32)
    for j, (s, l) in enumerate(parts[:-1]):
        state = jnp.where(j < place, jnp.exp(l) * state + s, state)
    return state


def log_before(parts, place):
    total = jnp.zeros((1, HD), F32)
    for j, (_, l) in enumerate(parts[:-1]):
        total = jnp.where(j < place, total + l, total)
    return total


def enter_body(place_ref, mine_ref, line_ref, wide_ref, send_ref):
    line = parts_of(line_ref)
    wide = parts_of(wide_ref)
    state = before(wide, place_ref[1])
    entering = jnp.exp(log_before(line, place_ref[0])) * state + before(line, place_ref[0])
    for j, (s, l) in enumerate(parts_of(mine_ref)):
        send_ref[j] = entering.astype(BF16)
        entering = jnp.exp(l) * entering + s


def raw_body(query_ref, log_ref, local_ref, enter_ref, raw_ref, square_ref):
    heads = query_ref.shape[1] // HD
    sums = block_sums(log_ref)
    ahead = jnp.zeros((1, HD), F32)
    for b, cum in enumerate(sums):
        rows = slice(b * BLK, (b + 1) * BLK)
        for h in range(heads):
            lanes = slice(h * HD, (h + 1) * HD)
            inter = dot(query_ref[rows, lanes], enter_ref[h], ((1,), (0,)))
            weight = jnp.exp(cum[:, h : h + 1] + ahead[:, h : h + 1])
            raw_ref[rows, lanes] = local_ref[rows, lanes] + weight * inter
        ahead = ahead + cum[BLK - 1 : BLK, :]
    raw = raw_ref[...]
    ones = jnp.ones((square_ref.shape[0], raw.shape[1]), F32)
    square_ref[...] = dot(ones, raw * raw, ((1,), (1,)), lax.Precision.HIGHEST)


def norm_body(columns, raw_ref, square_ref, gate_ref, gain_ref, out_ref):
    ones = jnp.ones((square_ref.shape[0], HD), F32)
    total = dot(square_ref[...], ones, ((0,), (0,)), lax.Precision.HIGHEST)
    scale = lax.rsqrt(total / columns + EPS)
    for h in range(raw_ref.shape[1] // HD):
        lanes = slice(h * HD, (h + 1) * HD)
        gate = jax.nn.sigmoid(gate_ref[:, lanes].astype(F32))
        out_ref[:, lanes] = (raw_ref[:, lanes] * scale * gain_ref[:, lanes] * gate).astype(BF16)


def lightning(lin_query, lin_key, lin_value, lin_gate, log_decay, norm_gain, place):
    tokens, features = lin_query.shape
    heads = features // HD
    shards = lax.axis_size("seq")
    peers = lax.axis_size("head")
    logs = jnp.pad(log_decay, ((0, 0), (0, HD - heads)))
    sent = jax.ShapeDtypeStruct((heads, HD + LOG_ROWS, HD), BF16)
    send, first = call(
        states_body,
        (sent, jax.ShapeDtypeStruct((heads, HD, HD), F32)),
        (lin_key, lin_value, logs),
        flops=4 * tokens * features * HD,
        moved=4 * tokens * features,
    )
    near = [[QUAD * g + j for j in range(QUAD)] for g in range(shards // QUAD)]
    span = QUAD * QUAD
    line = [
        [span * x + QUAD * a + b for a in range(QUAD)]
        for x in range(shards // span)
        for b in range(QUAD)
    ]
    wide = [[span * x + r for x in range(shards // span)] for r in range(span)]

    def swap(array, groups):
        return lax.all_to_all(array, "seq", 0, 0, axis_index_groups=groups, tiled=True)

    mine = swap(send, near)
    local = call(
        local_body,
        jax.ShapeDtypeStruct((tokens, features), F32),
        (lin_query, lin_key, lin_value, logs, first),
        flops=4 * tokens * features * BLK,
        moved=10 * tokens * features,
    )
    small = dict(flops=10 * heads * HD * HD, moved=4 * heads * HD * HD)
    lines = swap(call(group_body, sent, (mine,), **small), line)
    wides = swap(call(group_body, sent, (lines,), **small), wide)
    entering = call(
        enter_body,
        jax.ShapeDtypeStruct((heads, HD, HD), BF16),
        (place, mine, lines, wides),
        smem=(0,),
        **small,
    )
    entering = swap(entering, near)
    raw, squares = call(
        raw_body,
        (
            jax.ShapeDtypeStruct((tokens, features), F32),
            jax.ShapeDtypeStruct((peers, tokens), F32),
        ),
        (lin_query, logs, local, entering),
        flops=2 * tokens * features * HD,
        moved=10 * tokens * features,
    )
    squares = lax.all_to_all(squares, "head", 0, 0, tiled=True)
    return call(
        functools.partial(norm_body, float(features * peers)),
        jax.ShapeDtypeStruct((tokens, features), BF16),
        (raw, squares, lin_gate, norm_gain.reshape(1, features)),
        flops=8 * tokens * features,
        moved=8 * tokens * features,
        exps=tokens * features,
    )


SCALE = math.log2(math.e) * HD ** (-0.5)


def attend_body(own, first, count, final, *refs):
    refs = list(refs)
    place_ref, docs_ref, query_ref = refs[:3]
    pieces = refs[3 : 3 + count]
    rest = refs[3 + count :]
    if own:
        before_refs, rest = None, rest
    else:
        before_refs, rest = rest[:2], rest[2:]
    if final:
        out_ref, acc_ref, max_ref = rest
    else:
        acc_ref, max_ref = rest
    tokens, features = query_ref.shape
    heads = features // HD
    blocks = tokens // MBLK
    shard = place_ref[2]
    rows = heads * MBLK
    ones = jnp.ones((tokens, HD), BF16)

    def queries(i):
        return jnp.concatenate(
            [query_ref[i * MBLK : (i + 1) * MBLK, h * HD : (h + 1) * HD] for h in range(heads)],
            axis=0,
        )

    for i in range(blocks):
        mine = docs_ref[shard * blocks + i]
        at = slice(i * rows, (i + 1) * rows)
        if not own and final:
            acc_ref[at, :] = before_refs[0][at, :]
            max_ref[at, :] = before_refs[1][at, :]
        for p in range(count):
            back = first + p
            piece = pieces[p]
            start = jnp.int32(0)
            for b in range(blocks):
                where = (shard - back) * blocks + b
                other = docs_ref[jnp.maximum(where, 0)]
                if back == 0 and b >= i:
                    continue
                start = start + jnp.where((where >= 0) & (other == mine), 0, MBLK)
            if back == 0:
                width = (i + 1) * MBLK
                scores = dot(queries(i), piece[:width, :HD], ((1,), (1,))) * SCALE
                col = lax.broadcasted_iota(jnp.int32, (rows, width), 1)
                row = lax.broadcasted_iota(jnp.int32, (rows, width), 0)
                row = (row & (MBLK - 1)) + i * MBLK
                scores = jnp.where((col <= row) & (col >= start), scores, NEG)
                top = jnp.max(scores, axis=1, keepdims=True)
                probs = jnp.exp2(scores - top).astype(BF16)
                wide = jnp.concatenate([piece[:width, HD:], ones[:width]], axis=1)
                acc_ref[at, :] = dot(probs, wide, ((1,), (0,)))
                max_ref[at, :] = jnp.broadcast_to(top, (rows, HD))
            else:

                @pl.when(start < tokens)
                def _():
                    scores = dot(queries(i), piece[:, :HD], ((1,), (1,))) * SCALE
                    col = lax.broadcasted_iota(jnp.int32, (1, tokens), 1)
                    scores = scores + jnp.where(col >= start, 0.0, NEG)
                    old = max_ref[at, :]
                    top = jnp.maximum(old, jnp.max(scores, axis=1, keepdims=True))
                    shrink = jnp.exp2(old - top)
                    probs = jnp.exp2(scores - top[:, :1]).astype(BF16)
                    wide = jnp.concatenate([piece[:, HD:], ones], axis=1)
                    added = dot(probs, wide, ((1,), (0,)))
                    acc_ref[at, :HD] = acc_ref[at, :HD] * shrink + added[:, :HD]
                    acc_ref[at, HD:] = acc_ref[at, HD:] * shrink + added[:, HD:]
                    max_ref[at, :] = top

        if final:
            done = acc_ref[at, :HD] / acc_ref[at, HD:]
            for h in range(heads):
                out_ref[i * MBLK : (i + 1) * MBLK, h * HD : (h + 1) * HD] = done[
                    h * MBLK : (h + 1) * MBLK
                ].astype(BF16)


def attend(soft_query, soft_key, soft_value, doc_ids, place):
    tokens, features = soft_query.shape
    shards = lax.axis_size("seq")
    blocks = tokens // MBLK
    hops = (DOC_MOST + blocks - 2) // blocks
    heads = features // HD
    moving = jnp.concatenate([soft_key, soft_value], axis=1)
    pieces = [moving]
    for _ in range(hops):
        moving = lax.ppermute(moving, "seq", [(s, s + 1) for s in range(shards - 1)])
        pieces.append(moving)
    carry = (
        jax.ShapeDtypeStruct((heads * tokens, 2 * HD), F32),
        jax.ShapeDtypeStruct((heads * tokens, HD), F32),
    )
    state = ()
    cuts = (0, 2, 4, 6, hops + 1)
    for lo, hi in zip(cuts[:-1], cuts[1:]):
        final = hi == hops + 1
        operands = (place, doc_ids, soft_query, *pieces[lo:hi], *state)
        aliases = None
        if state and not final:
            aliases = {len(operands) - 2: 0, len(operands) - 1: 1}
        state = call(
            functools.partial(attend_body, lo == 0, lo, hi - lo, final),
            jax.ShapeDtypeStruct((tokens, features), BF16) if final else carry,
            operands,
            smem=(0, 1),
            aliases=aliases,
            scratch=tuple(pltpu.VMEM(c.shape, c.dtype) for c in carry) if final else (),
            flops=(hi - lo) * 4 * tokens * tokens * features,
            moved=12 * tokens * features,
            exps=(hi - lo) * heads * tokens * tokens,
        )
    return state


def on_device(
    lin_query,
    lin_key,
    lin_value,
    lin_gate,
    log_decay,
    norm_gain,
    soft_query,
    soft_key,
    soft_value,
    doc_ids,
):
    shard = lax.axis_index("seq")
    span = QUAD * QUAD
    place = jnp.stack([(shard % span) // QUAD, shard // span, shard]).astype(jnp.int32)
    soft_out = attend(soft_query, soft_key, soft_value, doc_ids, place)
    lin_out = lightning(lin_query, lin_key, lin_value, lin_gate, log_decay, norm_gain, place)
    return (lin_out, soft_out)


def solution(mesh):
    spread = P("seq", "head")
    return jax.shard_map(
        on_device,
        mesh=mesh,
        in_specs=(spread,) * 5 + (P("head"),) + (spread,) * 3 + (P(),),
        out_specs=(spread, spread),
        check_vma=False,
    )
```

time: 432 us -> 135 us (0.31)
  the two profiles are of different devices: /device:TPU:7 before, /device:TPU:367 now
where the time goes in v1:
time: 135 us; the launch traced here: 134 us
  starting transfers between devices  52.2 us (39%)
  Pallas kernels  45.4 us (34%)
  waiting for transfers between devices  18.3 us (14%)
  local copies, waits for them, and re-layouts  16.8 us (12%)
    pallas_call x11, Pallas kernels, call(): pl.pallas_call(body, out_shape=outs, in_specs=specs, out_specs=jax.tree.m...  45.4 us
    all_to_all x4, starting transfers between devices, swap(): lax.all_to_all(array, 'seq', 0, 0, axis_index_groups=groups, tiled=True)  24.8 us
    ppermute x7, starting transfers between devices, attend(): lax.ppermute(moving, 'seq', [(s, s + 1) for s in range(shards - 1)])  19 us
    ppermute x7, waiting for transfers between devices, attend(): lax.ppermute(moving, 'seq', [(s, s + 1) for s in range(shards - 1)])  16.2 us
    unnamed x59, local copies, waits for them, and re-layouts  15.2 us
    all_to_all x1, starting transfers between devices, lightning(): squares = lax.all_to_all(squares, 'head', 0, 0, tiled=True)  8.37 us
  transfers between devices with their start and end apart: 12, of which 4 were waited for; matrix products, arithmetic and copies ran while one was open for 1% of the time, Pallas kernels for 29%

profile of v1, /device:TPU:367, one launch (start us, length us, event | category | flops | bytes accessed | tf_op | source)
XLA Modules:
  0.0 133.8 jit_solution(2921405948685442784)
XLA Ops:
  2.5 2.6 %collective-permute-start = (bf16[512,256]{1,0:T(8,128)(2,1)S(1)}, bf16[512,256]{1,0:T(8,128)(2,1)S(1)}, u32[]{:S(2)}, u32[]{:S(2)}) collective-permute-start(bf16[512,256]{1,0:T(8,128)(2,1)S(1)} %constant_dynamic-update-slice_fusion.refs_3_), channel_id=1, source_target_pairs={{0,8},{8,16},{16,24},{24,32},{32,40},{40,48},{48,56},{56,64},{64,7... | collective-permute-start | bytes 786440 | tf_op jit(solution)/shard_map/ppermute | solution.py:361
  5.9 5.7 %collective-permute-done.refs_4_ = bf16[512,256]{1,0:T(8,128)(2,1)S(1)} collective-permute-done((bf16[512,256]{1,0:T(8,128)(2,1)S(1)}, bf16[512,256]{1,0:T(8,128)(2,1)S(1)}, u32[]{:S(2)}, u32[]{:S(2)}) %collective-permute-start) | collective-permute-done | bytes 262176 | tf_op jit(solution)/shard_map/ppermute | solution.py:361
  11.6 3.8 %collective-permute-start.1 = (bf16[512,256]{1,0:T(8,128)(2,1)S(1)}, bf16[512,256]{1,0:T(8,128)(2,1)S(1)}, u32[]{:S(2)}, u32[]{:S(2)}) collective-permute-start(bf16[512,256]{1,0:T(8,128)(2,1)S(1)} %collective-permute-done.refs_4_), channel_id=1, source_target_pairs={{0,8},{8,16},{16,24},{24,32},{32,40},{40,48},{48,56},{56,64},{64,7... | collective-permute-start | bytes 786440 | tf_op jit(solution)/shard_map/ppermute | solution.py:361
  18.5 2.1 %shard_map.113 = (bf16[4,144,128]{2,1,0:T(8,128)(2,1)}, f32[4,128,128]{2,1,0:T(8,128)S(1)}) custom-call(bf16[512,512]{1,0:T(8,128)(2,1)S(1)} %copy-done.5, bf16[512,512]{1,0:T(8,128)(2,1)S(1)} %copy-done.7, f32[512,128]{1,0:T(8,128)S(1)} %pad.4.log_ref), custom_call_target="tpu_custom_call" | custom-call | flops 134217728 | bytes 1048576 | tf_op jit(solution)/shard_map/pallas_call | solution.py:31
  20.6 4.5 %all-to-all-start = ((bf16[4,144,128]{2,1,0:T(8,128)(2,1)}), bf16[4,144,128]{2,1,0:T(8,128)(2,1)S(1)}, u32[]{:S(2)}, u32[]{:S(2)}) async-start(bf16[4,144,128]{2,1,0:T(8,128)(2,1)} %get-tuple-element.13), calls=%async_computation | async-start | bytes 294912 | tf_op jit(solution)/shard_map/all_to_all | solution.py:228
  25.1 1.9 %collective-permute-start.2 = (bf16[512,256]{1,0:T(8,128)(2,1)S(1)}, bf16[512,256]{1,0:T(8,128)(2,1)S(1)}, u32[]{:S(2)}, u32[]{:S(2)}) collective-permute-start(bf16[512,256]{1,0:T(8,128)(2,1)S(1)} %collective-permute-done.1.refs_3_), channel_id=1, source_target_pairs={{0,8},{8,16},{16,24},{24,32},{32,40},{40,48},{48,56},{56,64},{64,7... | collective-permute-start | bytes 786440 | tf_op jit(solution)/shard_map/ppermute | solution.py:361
  27.0 6.8 %collective-permute-done.2.refs_4_ = bf16[512,256]{1,0:T(8,128)(2,1)S(1)} collective-permute-done((bf16[512,256]{1,0:T(8,128)(2,1)S(1)}, bf16[512,256]{1,0:T(8,128)(2,1)S(1)}, u32[]{:S(2)}, u32[]{:S(2)}) %collective-permute-start.2) | collective-permute-done | bytes 262176 | tf_op jit(solution)/shard_map/ppermute | solution.py:361
  33.9 2.0 %collective-permute-start.3 = (bf16[512,256]{1,0:T(8,128)(2,1)S(1)}, bf16[512,256]{1,0:T(8,128)(2,1)S(1)}, u32[]{:S(2)}, u32[]{:S(2)}) collective-permute-start(bf16[512,256]{1,0:T(8,128)(2,1)S(1)} %collective-permute-done.2.refs_4_), channel_id=1, source_target_pairs={{0,8},{8,16},{16,24},{24,32},{32,40},{40,48},{48,56},{56,64},{64,7... | collective-permute-start | bytes 786440 | tf_op jit(solution)/shard_map/ppermute | solution.py:361
  36.6 11.4 %all-to-all-start.1 = ((bf16[4,144,128]{2,1,0:T(8,128)(2,1)}), bf16[4,144,128]{2,1,0:T(8,128)(2,1)S(1)}, u32[]{:S(2)}, u32[]{:S(2)}) async-start(bf16[4,144,128]{2,1,0:T(8,128)(2,1)} %shard_map.115), calls=%async_computation.1 | async-start | bytes 294912 | tf_op jit(solution)/shard_map/all_to_all | solution.py:228
  48.0 1.9 %collective-permute-start.4 = (bf16[512,256]{1,0:T(8,128)(2,1)S(1)}, bf16[512,256]{1,0:T(8,128)(2,1)S(1)}, u32[]{:S(2)}, u32[]{:S(2)}) collective-permute-start(bf16[512,256]{1,0:T(8,128)(2,1)S(1)} %collective-permute-done.3.refs_3_), channel_id=1, source_target_pairs={{0,8},{8,16},{16,24},{24,32},{32,40},{40,48},{48,56},{56,64},{64,7... | collective-permute-start | bytes 786440 | tf_op jit(solution)/shard_map/ppermute | solution.py:361
  50.0 2.1 %all-to-all-done.1.got_ref.line_ref = bf16[4,144,128]{2,1,0:T(8,128)(2,1)S(1)} async-done(((bf16[4,144,128]{2,1,0:T(8,128)(2,1)}), bf16[4,144,128]{2,1,0:T(8,128)(2,1)S(1)}, u32[]{:S(2)}, u32[]{:S(2)}) %all-to-all-start.1) | async-done | bytes 147488 | tf_op jit(solution)/shard_map/all_to_all | solution.py:228
  52.8 4.3 %all-to-all-start.2 = ((bf16[4,144,128]{2,1,0:T(8,128)(2,1)}), bf16[4,144,128]{2,1,0:T(8,128)(2,1)S(1)}, u32[]{:S(2)}, u32[]{:S(2)}) async-start(bf16[4,144,128]{2,1,0:T(8,128)(2,1)} %shard_map.116), calls=%async_computation.2 | async-start | bytes 294912 | tf_op jit(solution)/shard_map/all_to_all | solution.py:228
  57.1 3.7 %collective-permute-done.4.refs_4_ = bf16[512,256]{1,0:T(8,128)(2,1)S(1)} collective-permute-done((bf16[512,256]{1,0:T(8,128)(2,1)S(1)}, bf16[512,256]{1,0:T(8,128)(2,1)S(1)}, u32[]{:S(2)}, u32[]{:S(2)}) %collective-permute-start.4) | collective-permute-done | bytes 262176 | tf_op jit(solution)/shard_map/ppermute | solution.py:361
  60.8 4.8 %collective-permute-start.5 = (bf16[512,256]{1,0:T(8,128)(2,1)S(1)}, bf16[512,256]{1,0:T(8,128)(2,1)}, u32[]{:S(2)}, u32[]{:S(2)}) collective-permute-start(bf16[512,256]{1,0:T(8,128)(2,1)S(1)} %collective-permute-done.4.refs_4_), channel_id=1, source_target_pairs={{0,8},{8,16},{16,24},{24,32},{32,40},{40,48},{48,56},{56,64},{64,7... | collective-permute-start | bytes 786440 | tf_op jit(solution)/shard_map/ppermute | solution.py:361
  67.0 4.5 %all-to-all-start.3 = ((bf16[4,128,128]{2,1,0:T(8,128)(2,1)}), bf16[4,128,128]{2,1,0:T(8,128)(2,1)S(1)}, u32[]{:S(2)}, u32[]{:S(2)}) async-start(bf16[4,128,128]{2,1,0:T(8,128)(2,1)} %shard_map.117), calls=%async_computation.3 | async-start | bytes 262144 | tf_op jit(solution)/shard_map/all_to_all | solution.py:228
  71.6 1.6 %shard_map.114.local_ref = f32[512,512]{1,0:T(8,128)S(1)} custom-call(bf16[512,512]{1,0:T(8,128)(2,1)S(1)} %copy-done.9, bf16[512,512]{1,0:T(8,128)(2,1)S(1)} %copy-done.6, bf16[512,512]{1,0:T(8,128)(2,1)S(1)} %copy-done.8, f32[512,128]{1,0:T(8,128)S(1)} %pad.4.log_ref, f32[4,128,128]{2,1,0:T(8,128)S(1)} %get-tuple-element.12.first_ref), custom_call_target="tpu_custom_call" | custom-call | flops 268435456 | bytes 2621440 | tf_op jit(solution)/shard_map/pallas_call | solution.py:31
  73.2 1.9 %collective-permute-start.6 = (bf16[512,256]{1,0:T(8,128)(2,1)}, bf16[512,256]{1,0:T(8,128)(2,1)}, u32[]{:S(2)}, u32[]{:S(2)}) collective-permute-start(bf16[512,256]{1,0:T(8,128)(2,1)} %collective-permute-done.5.refs_3_), channel_id=1, source_target_pairs={{0,8},{8,16},{16,24},{24,32},{32,40},{40,48},{48,56},{56,64},{64,7... | collective-permute-start | bytes 786440 | tf_op jit(solution)/shard_map/ppermute | solution.py:361
  77.1 7.8 %shard_map.120 = (f32[2048,256]{1,0:T(8,128)S(1)}, f32[2048,128]{1,0:T(8,128)S(1)}) custom-call(s32[3]{0:T(128)S(1)} %pad_add_fusion.place_ref.refs_0_, s32[256]{0:T(256)S(1)} %copy-done.24, bf16[512,512]{1,0:T(8,128)(2,1)S(1)} %copy-done, bf16[512,256]{1,0:T(8,128)(2,1)S(1)} %copy-done.23, bf16[512,256]{1,0:T(8,128)(2,1)S(1)} %copy-done.27), custom_call_target="tpu_custom_call" | custom-call | flops 1073741824 | bytes 3145728 | tf_op jit(solution)/shard_map/pallas_call | solution.py:31
  85.0 10.5 %shard_map.121 = (f32[2048,256]{1,0:T(8,128)S(1)}, f32[2048,128]{1,0:T(8,128)S(1)}) custom-call(s32[3]{0:T(128)S(1)} %pad_add_fusion.place_ref.refs_0_, s32[256]{0:T(256)S(1)} %copy-done.24, bf16[512,512]{1,0:T(8,128)(2,1)S(1)} %copy-done, bf16[512,256]{1,0:T(8,128)(2,1)S(1)} %copy-done.15, ...), custom_call_target="tpu_custom_call", output_to_operand_aliasing={{0}: (5, {}), {1}: (6, {})} | custom-call | flops 1073741824 | bytes 3145728 | tf_op jit(solution)/shard_map/pallas_call | solution.py:31
  97.8 1.7 %shard_map.118 = (f32[512,512]{1,0:T(8,128)S(1)}, f32[8,512]{1,0:T(8,128)S(1)}) custom-call(bf16[512,512]{1,0:T(8,128)(2,1)S(1)} %copy-done.10, f32[512,128]{1,0:T(8,128)S(1)} %pad.4.log_ref, f32[512,512]{1,0:T(8,128)S(1)} %copy-done.4, bf16[4,128,128]{2,1,0:T(8,128)(2,1)S(1)} %all-to-all-done.3.enter_ref), custom_call_target="tpu_custom_call" | custom-call | flops 67108864 | bytes 2621440 | tf_op jit(solution)/shard_map/pallas_call | solution.py:31
  101.1 8.4 %all-to-all-start.4 = ((f32[8,1,512]{2,1,0:T(1,128)}), f32[8,1,512]{2,1,0:T(1,128)S(1)}, u32[]{:S(2)}, u32[]{:S(2)}) async-start(f32[8,1,512]{2,1,0:T(1,128)} %copy.18), calls=%async_computation.4 | async-start | bytes 32768 | tf_op jit(solution)/shard_map/all_to_all | solution.py:259
  112.4 10.5 %shard_map.122 = (f32[2048,256]{1,0:T(8,128)S(1)}, f32[2048,128]{1,0:T(8,128)S(1)}) custom-call(s32[3]{0:T(128)S(1)} %pad_add_fusion.place_ref.refs_0_, s32[256]{0:T(256)S(1)} %copy-done.24, bf16[512,512]{1,0:T(8,128)(2,1)S(1)} %copy-done.1, bf16[512,256]{1,0:T(8,128)(2,1)S(1)} %copy-done.17, ...), custom_call_target="tpu_custom_call", output_to_operand_aliasing={{0}: (5, {}), {1}: (6, {})} | custom-call | flops 1073741824 | bytes 3145728 | tf_op jit(solution)/shard_map/pallas_call | solution.py:31
  125.3 1.4 %shard_map.119 = bf16[512,512]{1,0:T(8,128)(2,1)} custom-call(f32[512,512]{1,0:T(8,128)S(1)} %copy-done.12, f32[8,512]{1,0:T(8,128)S(1)} %bitcast.8, bf16[512,512]{1,0:T(8,128)(2,1)S(1)} %copy-done.13, f32[1,512]{1,0:T(1,128)S(1)} %bitcast.10), custom_call_target="tpu_custom_call" | custom-call | flops 2097152 | bytes 2097152 | tf_op jit(solution)/shard_map/pallas_call | solution.py:31
  126.7 7.0 %shard_map.123 = bf16[512,512]{1,0:T(8,128)(2,1)} custom-call(s32[3]{0:T(128)S(1)} %pad_add_fusion.place_ref.refs_0_, s32[256]{0:T(256)S(1)} %copy-done.24, bf16[512,512]{1,0:T(8,128)(2,1)S(1)} %copy-done.2, bf16[512,256]{1,0:T(8,128)(2,1)} %collective-permute-done.5.refs_3_, bf16[512,256]{1,0:T(8,128)(2,1)} %collective-permute-done.6.refs_4_, ...), custom_call_target="tpu_custom_call" | custom-call | flops 1073741824 | bytes 3145728 | tf_op jit(solution)/shard_map/pallas_call | solution.py:31
  (74 shorter events, 19.6 us)
Async XLA Ops:
  2.5 9.1 %collective-permute-start = (bf16[512,256]{1,0:T(8,128)(2,1)S(1)}, bf16[512,256]{1,0:T(8,128)(2,1)S(1)}, u32[]{:S(2)}, u32[]{:S(2)}) collective-permute-start(bf16[512,256]{1,0:T(8,128)(2,1)S(1)} %constant_dynamic-update-slice_fusion.refs_3_), channel_id=1, source_target_pairs={{0,8},{8,16},{16,24},{24,32},{32,40},{40,48},{48,56},{56,64},{64,7... | collective-permute-start | bytes 786440 | tf_op jit(solution)/shard_map/ppermute | solution.py:361
  11.6 55.4 %copy-start.26 = (bf16[512,256]{1,0:T(8,128)(2,1)}, bf16[512,256]{1,0:T(8,128)(2,1)S(1)}, u32[]{:S(2)}) copy-start(bf16[512,256]{1,0:T(8,128)(2,1)S(1)} %collective-permute-done.refs_4_) | copy-start | bytes 786436
  11.6 13.5 %collective-permute-start.1 = (bf16[512,256]{1,0:T(8,128)(2,1)S(1)}, bf16[512,256]{1,0:T(8,128)(2,1)S(1)}, u32[]{:S(2)}, u32[]{:S(2)}) collective-permute-start(bf16[512,256]{1,0:T(8,128)(2,1)S(1)} %collective-permute-done.refs_4_), channel_id=1, source_target_pairs={{0,8},{8,16},{16,24},{24,32},{32,40},{40,48},{48,56},{56,64},{64,7... | collective-permute-start | bytes 786440 | tf_op jit(solution)/shard_map/ppermute | solution.py:361
  16.3 55.3 %copy-start.6 = (bf16[512,512]{1,0:T(8,128)(2,1)S(1)}, bf16[512,512]{1,0:T(8,128)(2,1)}, u32[]{:S(2)}) copy-start(bf16[512,512]{1,0:T(8,128)(2,1)} %key_ref.3) | copy-start | bytes 1572868
  18.5 53.1 %copy-start.8 = (bf16[512,512]{1,0:T(8,128)(2,1)S(1)}, bf16[512,512]{1,0:T(8,128)(2,1)}, u32[]{:S(2)}) copy-start(bf16[512,512]{1,0:T(8,128)(2,1)} %value_ref.3) | copy-start | bytes 1572868
  18.5 53.1 %copy-start.9 = (bf16[512,512]{1,0:T(8,128)(2,1)S(1)}, bf16[512,512]{1,0:T(8,128)(2,1)}, u32[]{:S(2)}) copy-start(bf16[512,512]{1,0:T(8,128)(2,1)} %query_ref.3) | copy-start | bytes 1572868
  20.6 15.3 %all-to-all-start = ((bf16[4,144,128]{2,1,0:T(8,128)(2,1)}), bf16[4,144,128]{2,1,0:T(8,128)(2,1)S(1)}, u32[]{:S(2)}, u32[]{:S(2)}) async-start(bf16[4,144,128]{2,1,0:T(8,128)(2,1)} %get-tuple-element.13), calls=%async_computation | async-start | bytes 294912 | tf_op jit(solution)/shard_map/all_to_all | solution.py:228
  25.1 11.4 %copy-start.14 = (bf16[512,256]{1,0:T(8,128)(2,1)}, bf16[512,256]{1,0:T(8,128)(2,1)S(1)}, u32[]{:S(2)}) copy-start(bf16[512,256]{1,0:T(8,128)(2,1)S(1)} %collective-permute-done.1.refs_3_) | copy-start | bytes 786436
  25.1 8.7 %collective-permute-start.2 = (bf16[512,256]{1,0:T(8,128)(2,1)S(1)}, bf16[512,256]{1,0:T(8,128)(2,1)S(1)}, u32[]{:S(2)}, u32[]{:S(2)}) collective-permute-start(bf16[512,256]{1,0:T(8,128)(2,1)S(1)} %collective-permute-done.1.refs_3_), channel_id=1, source_target_pairs={{0,8},{8,16},{16,24},{24,32},{32,40},{40,48},{48,56},{56,64},{64,7... | collective-permute-start | bytes 786440 | tf_op jit(solution)/shard_map/ppermute | solution.py:361
  33.9 14.2 %copy-start.20 = (bf16[512,256]{1,0:T(8,128)(2,1)}, bf16[512,256]{1,0:T(8,128)(2,1)S(1)}, u32[]{:S(2)}) copy-start(bf16[512,256]{1,0:T(8,128)(2,1)S(1)} %collective-permute-done.2.refs_4_) | copy-start | bytes 786436
  33.9 14.2 %collective-permute-start.3 = (bf16[512,256]{1,0:T(8,128)(2,1)S(1)}, bf16[512,256]{1,0:T(8,128)(2,1)S(1)}, u32[]{:S(2)}, u32[]{:S(2)}) collective-permute-start(bf16[512,256]{1,0:T(8,128)(2,1)S(1)} %collective-permute-done.2.refs_4_), channel_id=1, source_target_pairs={{0,8},{8,16},{16,24},{24,32},{32,40},{40,48},{48,56},{56,64},{64,7... | collective-permute-start | bytes 786440 | tf_op jit(solution)/shard_map/ppermute | solution.py:361
  36.6 15.5 %all-to-all-start.1 = ((bf16[4,144,128]{2,1,0:T(8,128)(2,1)}), bf16[4,144,128]{2,1,0:T(8,128)(2,1)S(1)}, u32[]{:S(2)}, u32[]{:S(2)}) async-start(bf16[4,144,128]{2,1,0:T(8,128)(2,1)} %shard_map.115), calls=%async_computation.1 | async-start | bytes 294912 | tf_op jit(solution)/shard_map/all_to_all | solution.py:228
  48.0 25.1 %copy-start.16 = (bf16[512,256]{1,0:T(8,128)(2,1)}, bf16[512,256]{1,0:T(8,128)(2,1)S(1)}, u32[]{:S(2)}) copy-start(bf16[512,256]{1,0:T(8,128)(2,1)S(1)} %collective-permute-done.3.refs_3_) | copy-start | bytes 786436
  48.0 12.8 %collective-permute-start.4 = (bf16[512,256]{1,0:T(8,128)(2,1)S(1)}, bf16[512,256]{1,0:T(8,128)(2,1)S(1)}, u32[]{:S(2)}, u32[]{:S(2)}) collective-permute-start(bf16[512,256]{1,0:T(8,128)(2,1)S(1)} %collective-permute-done.3.refs_3_), channel_id=1, source_target_pairs={{0,8},{8,16},{16,24},{24,32},{32,40},{40,48},{48,56},{56,64},{64,7... | collective-permute-start | bytes 786440 | tf_op jit(solution)/shard_map/ppermute | solution.py:361
  52.8 22.3 %copy-start.24 = (s32[256]{0:T(256)S(1)}, s32[256]{0:T(256)}, u32[]{:S(2)}) copy-start(s32[256]{0:T(256)} %refs_1_.7) | copy-start | bytes 3076
  52.8 12.9 %all-to-all-start.2 = ((bf16[4,144,128]{2,1,0:T(8,128)(2,1)}), bf16[4,144,128]{2,1,0:T(8,128)(2,1)S(1)}, u32[]{:S(2)}, u32[]{:S(2)}) async-start(bf16[4,144,128]{2,1,0:T(8,128)(2,1)} %shard_map.116), calls=%async_computation.2 | async-start | bytes 294912 | tf_op jit(solution)/shard_map/all_to_all | solution.py:228
  60.8 12.4 %copy-start.18 = (bf16[512,256]{1,0:T(8,128)(2,1)}, bf16[512,256]{1,0:T(8,128)(2,1)S(1)}, u32[]{:S(2)}) copy-start(bf16[512,256]{1,0:T(8,128)(2,1)S(1)} %collective-permute-done.4.refs_4_) | copy-start | bytes 786436
  60.8 12.3 %collective-permute-start.5 = (bf16[512,256]{1,0:T(8,128)(2,1)S(1)}, bf16[512,256]{1,0:T(8,128)(2,1)}, u32[]{:S(2)}, u32[]{:S(2)}) collective-permute-start(bf16[512,256]{1,0:T(8,128)(2,1)S(1)} %collective-permute-done.4.refs_4_), channel_id=1, source_target_pairs={{0,8},{8,16},{16,24},{24,32},{32,40},{40,48},{48,56},{56,64},{64,7... | collective-permute-start | bytes 786440 | tf_op jit(solution)/shard_map/ppermute | solution.py:361
  67.0 28.5 %all-to-all-start.3 = ((bf16[4,128,128]{2,1,0:T(8,128)(2,1)}), bf16[4,128,128]{2,1,0:T(8,128)(2,1)S(1)}, u32[]{:S(2)}, u32[]{:S(2)}) async-start(bf16[4,128,128]{2,1,0:T(8,128)(2,1)} %shard_map.117), calls=%async_computation.3 | async-start | bytes 262144 | tf_op jit(solution)/shard_map/all_to_all | solution.py:228
  71.5 13.4 %copy-start.15 = (bf16[512,256]{1,0:T(8,128)(2,1)S(1)}, bf16[512,256]{1,0:T(8,128)(2,1)}, u32[]{:S(2)}) copy-start(bf16[512,256]{1,0:T(8,128)(2,1)} %copy-done.14) | copy-start | bytes 786436
  71.5 13.4 %copy-start.21 = (bf16[512,256]{1,0:T(8,128)(2,1)S(1)}, bf16[512,256]{1,0:T(8,128)(2,1)}, u32[]{:S(2)}) copy-start(bf16[512,256]{1,0:T(8,128)(2,1)} %copy-done.20) | copy-start | bytes 786436
  73.2 11.8 %copy-start.3 = (f32[512,512]{1,0:T(8,128)}, f32[512,512]{1,0:T(8,128)S(1)}, u32[]{:S(2)}) copy-start(f32[512,512]{1,0:T(8,128)S(1)} %shard_map.114.local_ref) | copy-start | bytes 3145732
  73.2 53.5 %collective-permute-start.6 = (bf16[512,256]{1,0:T(8,128)(2,1)}, bf16[512,256]{1,0:T(8,128)(2,1)}, u32[]{:S(2)}, u32[]{:S(2)}) collective-permute-start(bf16[512,256]{1,0:T(8,128)(2,1)} %collective-permute-done.5.refs_3_), channel_id=1, source_target_pairs={{0,8},{8,16},{16,24},{24,32},{32,40},{40,48},{48,56},{56,64},{64,7... | collective-permute-start | bytes 786440 | tf_op jit(solution)/shard_map/ppermute | solution.py:361
  101.1 21.8 %all-to-all-start.4 = ((f32[8,1,512]{2,1,0:T(1,128)}), f32[8,1,512]{2,1,0:T(1,128)S(1)}, u32[]{:S(2)}, u32[]{:S(2)}) async-start(f32[8,1,512]{2,1,0:T(1,128)} %copy.18), calls=%async_computation.4 | async-start | bytes 32768 | tf_op jit(solution)/shard_map/all_to_all | solution.py:259
  (16 other events, 31.4 us)

commit v2 on v1

--- a/solution.py
+++ b/solution.py
@@ -21,6 +21,7 @@
 F32 = jnp.float32
 BF16 = jnp.bfloat16
 VMEM_LIMIT = 48 * 1024 * 1024
+COST = 4 * 10**9
 
 
 def call(body, outs, operands, *, flops, moved, exps=0, scratch=(), smem=(), aliases=None):
@@ -72,7 +73,9 @@
     return packed.astype(BF16)
 
 
-def states_body(key_ref, value_ref, log_ref, send_ref, first_ref):
+def states_body(key_ref, value_ref, log_ref, soft_key_ref, soft_value_ref, send_ref, first_ref, moving_ref):
+    moving_ref[:, : soft_key_ref.shape[1]] = soft_key_ref[...]
+    moving_ref[:, soft_key_ref.shape[1] :] = soft_value_ref[...]
     heads = key_ref.shape[1] // HD
     sums = block_sums(log_ref)
     ends = [s[BLK - 1 : BLK, :] for s in sums]
@@ -143,8 +146,11 @@
 
 def group_body(got_ref, send_ref):
     state, total = fold(parts_of(got_ref))
-    state = state.astype(BF16)
+    state = state.astype(send_ref.dtype)
     rows = log_rows(total)
+    if send_ref.dtype == F32:
+        row = lax.broadcasted_iota(jnp.int32, (send_ref.shape[1] - HD, HD), 0)
+        rows = jnp.where(row == 0, total, 0.0)
     for j in range(send_ref.shape[0]):
         send_ref[j, :HD, :] = state
         send_ref[j, HD:, :] = rows
@@ -201,20 +207,29 @@
         out_ref[:, lanes] = (raw_ref[:, lanes] * scale * gain_ref[:, lanes] * gate).astype(BF16)
 
 
-def lightning(lin_query, lin_key, lin_value, lin_gate, log_decay, norm_gain, place):
+def states(lin_key, lin_value, log_decay, soft_key, soft_value):
+    tokens, features = lin_key.shape
+    heads = features // HD
+    logs = jnp.pad(log_decay, ((0, 0), (0, HD - heads)))
+    send, first, moving = call(
+        states_body,
+        (
+            jax.ShapeDtypeStruct((heads, HD + LOG_ROWS, HD), BF16),
+            jax.ShapeDtypeStruct((heads, HD, HD), F32),
+            jax.ShapeDtypeStruct((tokens, 2 * soft_key.shape[1]), BF16),
+        ),
+        (lin_key, lin_value, logs, soft_key, soft_value),
+        flops=4 * tokens * features * HD,
+        moved=4 * tokens * features,
+    )
+    return logs, send, first, moving
+
+
+def lightning(lin_query, lin_key, lin_value, lin_gate, logs, send, first, norm_gain, place):
     tokens, features = lin_query.shape
     heads = features // HD
     shards = lax.axis_size("seq")
     peers = lax.axis_size("head")
-    logs = jnp.pad(log_decay, ((0, 0), (0, HD - heads)))
-    sent = jax.ShapeDtypeStruct((heads, HD + LOG_ROWS, HD), BF16)
-    send, first = call(
-        states_body,
-        (sent, jax.ShapeDtypeStruct((heads, HD, HD), F32)),
-        (lin_key, lin_value, logs),
-        flops=4 * tokens * features * HD,
-        moved=4 * tokens * features,
-    )
     near = [[QUAD * g + j for j in range(QUAD)] for g in range(shards // QUAD)]
     span = QUAD * QUAD
     line = [
@@ -236,8 +251,10 @@
         moved=10 * tokens * features,
     )
     small = dict(flops=10 * heads * HD * HD, moved=4 * heads * HD * HD)
+    sent = jax.ShapeDtypeStruct((QUAD, HD + LOG_ROWS, HD), BF16)
+    exact = jax.ShapeDtypeStruct((shards // span, HD + 8, HD), F32)
     lines = swap(call(group_body, sent, (mine,), **small), line)
-    wides = swap(call(group_body, sent, (lines,), **small), wide)
+    wides = swap(call(group_body, exact, (lines,), **small), wide)
     entering = call(
         enter_body,
         jax.ShapeDtypeStruct((heads, HD, HD), BF16),
@@ -270,118 +287,121 @@
 SCALE = math.log2(math.e) * HD ** (-0.5)
 
 
-def attend_body(own, first, count, final, *refs):
+def attend_body(backs, opening, final, *refs):
     refs = list(refs)
     place_ref, docs_ref, query_ref = refs[:3]
-    pieces = refs[3 : 3 + count]
-    rest = refs[3 + count :]
-    if own:
-        before_refs, rest = None, rest
-    else:
-        before_refs, rest = rest[:2], rest[2:]
-    if final:
-        out_ref, acc_ref, max_ref = rest
-    else:
-        acc_ref, max_ref = rest
+    pieces = refs[3 : 3 + len(backs)]
+    rest = refs[3 + len(backs) :]
     tokens, features = query_ref.shape
     heads = features // HD
     blocks = tokens // MBLK
+    rows = heads * MBLK
     shard = place_ref[2]
-    rows = heads * MBLK
-    ones = jnp.ones((tokens, HD), BF16)
-
-    def queries(i):
-        return jnp.concatenate(
-            [query_ref[i * MBLK : (i + 1) * MBLK, h * HD : (h + 1) * HD] for h in range(heads)],
-            axis=0,
-        )
+    if opening:
+        acc_ref, top_ref, sum_ref = rest
+    elif final:
+        acc_in, top_in, sum_in, out_ref, acc_ref, top_ref, sum_ref = rest
+        acc_ref[...] = acc_in[...]
+        top_ref[...] = top_in[...]
+        sum_ref[...] = sum_in[...]
+    else:
+        acc_ref, top_ref, sum_ref = rest[3:]
 
     for i in range(blocks):
         mine = docs_ref[shard * blocks + i]
-        at = slice(i * rows, (i + 1) * rows)
-        if not own and final:
-            acc_ref[at, :] = before_refs[0][at, :]
-            max_ref[at, :] = before_refs[1][at, :]
-        for p in range(count):
-            back = first + p
-            piece = pieces[p]
+
+        def queries():
+            return jnp.concatenate(
+                [query_ref[i * MBLK : (i + 1) * MBLK, h * HD : (h + 1) * HD] for h in range(heads)],
+                axis=0,
+            )
+
+        for back, piece in zip(backs, pieces):
             start = jnp.int32(0)
-            for b in range(blocks):
+            for b in range(i if back == 0 else blocks):
                 where = (shard - back) * blocks + b
                 other = docs_ref[jnp.maximum(where, 0)]
-                if back == 0 and b >= i:
-                    continue
                 start = start + jnp.where((where >= 0) & (other == mine), 0, MBLK)
             if back == 0:
                 width = (i + 1) * MBLK
-                scores = dot(queries(i), piece[:width, :HD], ((1,), (1,))) * SCALE
-                col = lax.broadcasted_iota(jnp.int32, (rows, width), 1)
-                row = lax.broadcasted_iota(jnp.int32, (rows, width), 0)
-                row = (row & (MBLK - 1)) + i * MBLK
-                scores = jnp.where((col <= row) & (col >= start), scores, NEG)
-                top = jnp.max(scores, axis=1, keepdims=True)
-                probs = jnp.exp2(scores - top).astype(BF16)
-                wide = jnp.concatenate([piece[:width, HD:], ones[:width]], axis=1)
-                acc_ref[at, :] = dot(probs, wide, ((1,), (0,)))
-                max_ref[at, :] = jnp.broadcast_to(top, (rows, HD))
-            else:
-
-                @pl.when(start < tokens)
-                def _():
-                    scores = dot(queries(i), piece[:, :HD], ((1,), (1,))) * SCALE
-                    col = lax.broadcasted_iota(jnp.int32, (1, tokens), 1)
-                    scores = scores + jnp.where(col >= start, 0.0, NEG)
-                    old = max_ref[at, :]
-                    top = jnp.maximum(old, jnp.max(scores, axis=1, keepdims=True))
-                    shrink = jnp.exp2(old - top)
-                    probs = jnp.exp2(scores - top[:, :1]).astype(BF16)
-                    wide = jnp.concatenate([piece[:, HD:], ones], axis=1)
-                    added = dot(probs, wide, ((1,), (0,)))
-                    acc_ref[at, :HD] = acc_ref[at, :HD] * shrink + added[:, :HD]
-                    acc_ref[at, HD:] = acc_ref[at, HD:] * shrink + added[:, HD:]
-                    max_ref[at, :] = top
+                scores = dot(piece[:width, :HD], queries(), ((1,), (1,)))
+                key = lax.broadcasted_iota(jnp.int32, (width, rows), 0)
+                token = lax.broadcasted_iota(jnp.int32, (width, rows), 1)
+                token = (token & (MBLK - 1)) + i * MBLK
+                scores = jnp.where((key <= token) & (key >= start), scores, NEG)
+                top = jnp.max(scores, axis=0, keepdims=True)
+                probs = jnp.exp2(scores * SCALE - top * SCALE)
+                sum_ref[i] = jnp.sum(probs, axis=0, keepdims=True)
+                acc_ref[i] = dot(piece[:width, HD:], probs.astype(BF16), ((0,), (0,)))
+                top_ref[i] = top
+                continue
+
+            def add(masked):
+                scores = dot(piece[:, :HD], queries(), ((1,), (1,)))
+                if masked:
+                    key = lax.broadcasted_iota(jnp.int32, (tokens, rows), 0)
+                    scores = jnp.where(key >= start, scores, NEG)
+                old = top_ref[i]
+                top = jnp.maximum(old, jnp.max(scores, axis=0, keepdims=True))
+                probs = jnp.exp2(scores * SCALE - top * SCALE)
+                shrink = jnp.exp2((old - top) * SCALE)
+                sum_ref[i] = sum_ref[i] * shrink + jnp.sum(probs, axis=0, keepdims=True)
+                added = dot(piece[:, HD:], probs.astype(BF16), ((0,), (0,)))
+                acc_ref[i] = acc_ref[i] * shrink + added
+                top_ref[i] = top
+
+            pl.when(start == 0)(functools.partial(add, False))
+            pl.when((start > 0) & (start < tokens))(functools.partial(add, True))
 
         if final:
-            done = acc_ref[at, :HD] / acc_ref[at, HD:]
+            done = (acc_ref[i] / sum_ref[i]).T
             for h in range(heads):
                 out_ref[i * MBLK : (i + 1) * MBLK, h * HD : (h + 1) * HD] = done[
                     h * MBLK : (h + 1) * MBLK
                 ].astype(BF16)
 
 
-def attend(soft_query, soft_key, soft_value, doc_ids, place):
+def forward(array, steps):
+    shards = lax.axis_size("seq")
+    return lax.ppermute(array, "seq", [(s, s + steps) for s in range(shards - steps)])
+
+
+def attend(soft_query, own, doc_ids, place):
     tokens, features = soft_query.shape
-    shards = lax.axis_size("seq")
     blocks = tokens // MBLK
     hops = (DOC_MOST + blocks - 2) // blocks
     heads = features // HD
-    moving = jnp.concatenate([soft_key, soft_value], axis=1)
-    pieces = [moving]
-    for _ in range(hops):
-        moving = lax.ppermute(moving, "seq", [(s, s + 1) for s in range(shards - 1)])
-        pieces.append(moving)
+    half = (hops + 1) // 2
+    pieces = {0: own, half: forward(own, half)}
+    for back in range(1, half):
+        pieces[back] = forward(pieces[back - 1], 1)
+    for back in range(half + 1, hops + 1):
+        pieces[back] = forward(pieces[back - 1], 1)
+    rows = heads * MBLK
     carry = (
-        jax.ShapeDtypeStruct((heads * tokens, 2 * HD), F32),
-        jax.ShapeDtypeStruct((heads * tokens, HD), F32),
-    )
+        jax.ShapeDtypeStruct((blocks, HD, rows), F32),
+        jax.ShapeDtypeStruct((blocks, 1, rows), F32),
+        jax.ShapeDtypeStruct((blocks, 1, rows), F32),
+    )
+    calls = [(0,)] + [(b, b + half - 1) for b in range(1, half)]
+    calls.append(tuple(range(2 * half - 1, hops + 1)))
     state = ()
-    cuts = (0, 2, 4, 6, hops + 1)
-    for lo, hi in zip(cuts[:-1], cuts[1:]):
-        final = hi == hops + 1
-        operands = (place, doc_ids, soft_query, *pieces[lo:hi], *state)
+    for backs in calls:
+        opening, final = backs == calls[0], backs == calls[-1]
+        operands = (place, doc_ids, soft_query, *(pieces[b] for b in backs), *state)
         aliases = None
-        if state and not final:
-            aliases = {len(operands) - 2: 0, len(operands) - 1: 1}
+        if not opening and not final:
+            aliases = {len(operands) - 3 + j: j for j in range(3)}
         state = call(
-            functools.partial(attend_body, lo == 0, lo, hi - lo, final),
+            functools.partial(attend_body, backs, opening, final),
             jax.ShapeDtypeStruct((tokens, features), BF16) if final else carry,
             operands,
             smem=(0, 1),
             aliases=aliases,
             scratch=tuple(pltpu.VMEM(c.shape, c.dtype) for c in carry) if final else (),
-            flops=(hi - lo) * 4 * tokens * tokens * features,
+            flops=len(backs) * COST,
             moved=12 * tokens * features,
-            exps=(hi - lo) * heads * tokens * tokens,
+            exps=len(backs) * heads * tokens * tokens,
         )
     return state
 
@@ -401,8 +421,11 @@
     shard = lax.axis_index("seq")
     span = QUAD * QUAD
     place = jnp.stack([(shard % span) // QUAD, shard // span, shard]).astype(jnp.int32)
-    soft_out = attend(soft_query, soft_key, soft_value, doc_ids, place)
-    lin_out = lightning(lin_query, lin_key, lin_value, lin_gate, log_decay, norm_gain, place)
+    logs, send, first, moving = states(lin_key, lin_value, log_decay, soft_key, soft_value)
+    soft_out = attend(soft_query, moving, doc_ids, place)
+    lin_out = lightning(
+        lin_query, lin_key, lin_value, lin_gate, logs, send, first, norm_gain, place
+    )
     return (lin_out, soft_out)
 
 

time: 135 us -> 124 us (0.919)
  the two profiles are of different devices: /device:TPU:367 before, /device:TPU:45 now
where the time goes in v2:
time: 124 us; the launch traced here: 123 us
  starting transfers between devices  64.7 us (52%)
  Pallas kernels  37.6 us (30%)
  local copies, waits for them, and re-layouts  14.1 us (11%)
  waiting for transfers between devices  5.18 us (4%)
    pallas_call x12, Pallas kernels, call(): pl.pallas_call(body, out_shape=outs, in_specs=specs, out_specs=jax.tree.m...  37.6 us
    ppermute x7, starting transfers between devices, forward(): lax.ppermute(array, 'seq', [(s, s + steps) for s in range(shards - steps)])  30 us
    all_to_all x4, starting transfers between devices, swap(): lax.all_to_all(array, 'seq', 0, 0, axis_index_groups=groups, tiled=True)  26.9 us
    unnamed x42, local copies, waits for them, and re-layouts  13.5 us
    all_to_all x1, starting transfers between devices, lightning(): squares = lax.all_to_all(squares, 'head', 0, 0, tiled=True)  7.85 us
    ppermute x7, waiting for transfers between devices, forward(): lax.ppermute(array, 'seq', [(s, s + steps) for s in range(shards - steps)])  5.15 us
  transfers between devices with their start and end apart: 12, of which 2 were waited for; matrix products, arithmetic and copies ran while one was open for 1% of the time, Pallas kernels for 28%

profile of v2, /device:TPU:45, one launch (start us, length us, event | category | flops | bytes accessed | tf_op | source)
XLA Modules:
  0.0 122.5 jit_solution(2045214530304547412)
XLA Ops:
  3.6 2.2 %shard_map.113 = (bf16[4,144,128]{2,1,0:T(8,128)(2,1)}, f32[4,128,128]{2,1,0:T(8,128)S(1)}, bf16[512,256]{1,0:T(8,128)(2,1)}) custom-call(bf16[512,512]{1,0:T(8,128)(2,1)S(1)} %copy-done, bf16[512,512]{1,0:T(8,128)(2,1)S(1)} %copy-done.1, f32[512,128]{1,0:T(8,128)S(1)} %pad.4.log_ref, bf16[512,128]{1,0:T(8,128)(2,1)S(1)} %copy-done.5, ...), custom_call_target="tpu_custom_call" | custom-call | flops 134217728 | bytes 1048576 | tf_op jit(solution)/shard_map/pallas_call | solution.py:32
  5.7 8.8 %collective-permute-start = (bf16[512,256]{1,0:T(8,128)(2,1)}, bf16[512,256]{1,0:T(8,128)(2,1)}, u32[]{:S(2)}, u32[]{:S(2)}) collective-permute-start(bf16[512,256]{1,0:T(8,128)(2,1)} %get-tuple-element.23.refs_3_), channel_id=1, source_target_pairs={{0,32},{8,40},{16,48},{24,56},{32,64},{40,72},{48,80},{56,88},{64,... | collective-permute-start | bytes 786440 | tf_op jit(solution)/shard_map/ppermute | solution.py:366
  14.6 3.5 %collective-permute-start.4 = (bf16[512,256]{1,0:T(8,128)(2,1)}, bf16[512,256]{1,0:T(8,128)(2,1)}, u32[]{:S(2)}, u32[]{:S(2)}) collective-permute-start(bf16[512,256]{1,0:T(8,128)(2,1)} %get-tuple-element.23.refs_3_), channel_id=1, source_target_pairs={{0,8},{8,16},{16,24},{24,32},{32,40},{40,48},{48,56},{56,64},{64,7... | collective-permute-start | bytes 786440 | tf_op jit(solution)/shard_map/ppermute | solution.py:366
  18.1 6.7 %all-to-all-start = ((bf16[4,144,128]{2,1,0:T(8,128)(2,1)}), bf16[4,144,128]{2,1,0:T(8,128)(2,1)S(1)}, u32[]{:S(2)}, u32[]{:S(2)}) async-start(bf16[4,144,128]{2,1,0:T(8,128)(2,1)} %get-tuple-element.20), calls=%async_computation | async-start | bytes 294912 | tf_op jit(solution)/shard_map/all_to_all | solution.py:243
  24.9 1.6 %shard_map.114.local_ref = f32[512,512]{1,0:T(8,128)S(1)} custom-call(bf16[512,512]{1,0:T(8,128)(2,1)S(1)} %copy-done.3, bf16[512,512]{1,0:T(8,128)(2,1)S(1)} %copy-done, bf16[512,512]{1,0:T(8,128)(2,1)S(1)} %copy-done.2, f32[512,128]{1,0:T(8,128)S(1)} %pad.4.log_ref, f32[4,128,128]{2,1,0:T(8,128)S(1)} %get-tuple-element.19.first_ref), custom_call_target="tpu_custom_call" | custom-call | flops 268435456 | bytes 2621440 | tf_op jit(solution)/shard_map/pallas_call | solution.py:32
  26.5 2.8 %shard_map.120 = (f32[4,128,512]{2,1,0:T(8,128)S(1)}, f32[4,1,512]{2,1,0:T(1,128)S(1)}, f32[4,1,512]{2,1,0:T(1,128)S(1)}) custom-call(s32[3]{0:T(128)S(1)} %pad_add_fusion.place_ref.refs_0_, s32[256]{0:T(256)S(1)} %copy-done.11, bf16[512,512]{1,0:T(8,128)(2,1)S(1)} %copy-done.8, bf16[512,256]{1,0:T(8,128)(2,1)} %get-tuple-element.23.refs_3_), custom_call_target="tpu_custom_call" | custom-call | flops 4000000000 | bytes 3145728 | tf_op jit(solution)/shard_map/pallas_call | solution.py:32
  30.3 2.4 %collective-permute-done.refs_4_ = bf16[512,256]{1,0:T(8,128)(2,1)} collective-permute-done((bf16[512,256]{1,0:T(8,128)(2,1)}, bf16[512,256]{1,0:T(8,128)(2,1)}, u32[]{:S(2)}, u32[]{:S(2)}) %collective-permute-start) | collective-permute-done | bytes 262176 | tf_op jit(solution)/shard_map/ppermute | solution.py:366
  32.7 7.6 %collective-permute-start.1 = (bf16[512,256]{1,0:T(8,128)(2,1)}, bf16[512,256]{1,0:T(8,128)(2,1)}, u32[]{:S(2)}, u32[]{:S(2)}) collective-permute-start(bf16[512,256]{1,0:T(8,128)(2,1)} %collective-permute-done.refs_4_), channel_id=1, source_target_pairs={{0,8},{8,16},{16,24},{24,32},{32,40},{40,48},{48,56},{56,64},{64,7... | collective-permute-start | bytes 786440 | tf_op jit(solution)/shard_map/ppermute | solution.py:366
  40.3 2.7 %collective-permute-done.4.refs_3_ = bf16[512,256]{1,0:T(8,128)(2,1)} collective-permute-done((bf16[512,256]{1,0:T(8,128)(2,1)}, bf16[512,256]{1,0:T(8,128)(2,1)}, u32[]{:S(2)}, u32[]{:S(2)}) %collective-permute-start.4) | collective-permute-done | bytes 262176 | tf_op jit(solution)/shard_map/ppermute | solution.py:366
  43.0 4.3 %collective-permute-start.5 = (bf16[512,256]{1,0:T(8,128)(2,1)}, bf16[512,256]{1,0:T(8,128)(2,1)}, u32[]{:S(2)}, u32[]{:S(2)}) collective-permute-start(bf16[512,256]{1,0:T(8,128)(2,1)} %collective-permute-done.4.refs_3_), channel_id=1, source_target_pairs={{0,8},{8,16},{16,24},{24,32},{32,40},{40,48},{48,56},{56,64},{64,7... | collective-permute-start | bytes 786440 | tf_op jit(solution)/shard_map/ppermute | solution.py:366
  48.0 8.9 %all-to-all-start.1 = ((bf16[4,144,128]{2,1,0:T(8,128)(2,1)}), bf16[4,144,128]{2,1,0:T(8,128)(2,1)S(1)}, u32[]{:S(2)}, u32[]{:S(2)}) async-start(bf16[4,144,128]{2,1,0:T(8,128)(2,1)} %shard_map.115), calls=%async_computation.1 | async-start | bytes 294912 | tf_op jit(solution)/shard_map/all_to_all | solution.py:243
  58.1 6.8 %shard_map.121 = (f32[4,128,512]{2,1,0:T(8,128)S(1)}, f32[4,1,512]{2,1,0:T(1,128)S(1)}, f32[4,1,512]{2,1,0:T(1,128)S(1)}) custom-call(s32[3]{0:T(128)S(1)} %pad_add_fusion.place_ref.refs_0_, s32[256]{0:T(256)S(1)} %copy-done.11, bf16[512,512]{1,0:T(8,128)(2,1)S(1)} %copy-done.9, ...), custom_call_target="tpu_custom_call", output_to_operand_aliasing={{0}: (5, {}), {1}: (6, {}), {2}: (7, {})} | custom-call | flops 8000000000 | bytes 3145728 | tf_op jit(solution)/shard_map/pallas_call | solution.py:32
  65.9 1.9 %collective-permute-start.2 = (bf16[512,256]{1,0:T(8,128)(2,1)}, bf16[512,256]{1,0:T(8,128)(2,1)S(1)}, u32[]{:S(2)}, u32[]{:S(2)}) collective-permute-start(bf16[512,256]{1,0:T(8,128)(2,1)} %collective-permute-done.1.refs_4_), channel_id=1, source_target_pairs={{0,8},{8,16},{16,24},{24,32},{32,40},{40,48},{48,56},{56,64},{64,7... | collective-permute-start | bytes 786440 | tf_op jit(solution)/shard_map/ppermute | solution.py:366
  67.9 1.9 %collective-permute-start.6 = (bf16[512,256]{1,0:T(8,128)(2,1)}, bf16[512,256]{1,0:T(8,128)(2,1)}, u32[]{:S(2)}, u32[]{:S(2)}) collective-permute-start(bf16[512,256]{1,0:T(8,128)(2,1)} %collective-permute-done.5.refs_3_), channel_id=1, source_target_pairs={{0,8},{8,16},{16,24},{24,32},{32,40},{40,48},{48,56},{56,64},{64,7... | collective-permute-start | bytes 786440 | tf_op jit(solution)/shard_map/ppermute | solution.py:366
  70.6 4.2 %all-to-all-start.2 = ((f32[4,136,128]{2,1,0:T(8,128)}), f32[4,136,128]{2,1,0:T(8,128)S(1)}, u32[]{:S(2)}, u32[]{:S(2)}) async-start(f32[4,136,128]{2,1,0:T(8,128)} %shard_map.116), calls=%async_computation.2 | async-start | bytes 557056 | tf_op jit(solution)/shard_map/all_to_all | solution.py:243
  76.0 6.6 %shard_map.122 = (f32[4,128,512]{2,1,0:T(8,128)S(1)}, f32[4,1,512]{2,1,0:T(1,128)S(1)}, f32[4,1,512]{2,1,0:T(1,128)S(1)}) custom-call(s32[3]{0:T(128)S(1)} %pad_add_fusion.place_ref.refs_0_, s32[256]{0:T(256)S(1)} %copy-done.11, bf16[512,512]{1,0:T(8,128)(2,1)S(1)} %copy-done.9, ...), custom_call_target="tpu_custom_call", output_to_operand_aliasing={{0}: (5, {}), {1}: (6, {}), {2}: (7, {})} | custom-call | flops 8000000000 | bytes 3145728 | tf_op jit(solution)/shard_map/pallas_call | solution.py:32
  83.6 1.9 %collective-permute-start.3 = (bf16[512,256]{1,0:T(8,128)(2,1)S(1)}, bf16[512,256]{1,0:T(8,128)(2,1)}, u32[]{:S(2)}, u32[]{:S(2)}) collective-permute-start(bf16[512,256]{1,0:T(8,128)(2,1)S(1)} %collective-permute-done.2.refs_4_), channel_id=1, source_target_pairs={{0,8},{8,16},{16,24},{24,32},{32,40},{40,48},{48,56},{56,64},{64,7... | collective-permute-start | bytes 786440 | tf_op jit(solution)/shard_map/ppermute | solution.py:366
  85.6 1.3 %shard_map.117 = bf16[4,128,128]{2,1,0:T(8,128)(2,1)} custom-call(s32[3]{0:T(128)S(1)} %pad_add_fusion.place_ref.refs_0_, bf16[4,144,128]{2,1,0:T(8,128)(2,1)S(1)} %all-to-all-done.got_ref.mine_ref, bf16[4,144,128]{2,1,0:T(8,128)(2,1)S(1)} %all-to-all-done.1.got_ref.line_ref, f32[4,136,128]{2,1,0:T(8,128)S(1)} %all-to-all-done.2.wide_ref), custom_call_target="tpu_custom_call" | custom-call | flops 655360 | bytes 262144 | tf_op jit(solution)/shard_map/pallas_call | solution.py:32
  86.9 7.1 %all-to-all-start.3 = ((bf16[4,128,128]{2,1,0:T(8,128)(2,1)}), bf16[4,128,128]{2,1,0:T(8,128)(2,1)S(1)}, u32[]{:S(2)}, u32[]{:S(2)}) async-start(bf16[4,128,128]{2,1,0:T(8,128)(2,1)} %shard_map.117), calls=%async_computation.3 | async-start | bytes 262144 | tf_op jit(solution)/shard_map/all_to_all | solution.py:243
  95.2 6.8 %shard_map.123 = (f32[4,128,512]{2,1,0:T(8,128)S(1)}, f32[4,1,512]{2,1,0:T(1,128)S(1)}, f32[4,1,512]{2,1,0:T(1,128)S(1)}) custom-call(s32[3]{0:T(128)S(1)} %pad_add_fusion.place_ref.refs_0_, s32[256]{0:T(256)S(1)} %copy-done.11, bf16[512,512]{1,0:T(8,128)(2,1)S(1)} %copy-done.9, ...), custom_call_target="tpu_custom_call", output_to_operand_aliasing={{0}: (5, {}), {1}: (6, {}), {2}: (7, {})} | custom-call | flops 8000000000 | bytes 3145728 | tf_op jit(solution)/shard_map/pallas_call | solution.py:32
  102.9 1.7 %shard_map.118 = (f32[512,512]{1,0:T(8,128)S(1)}, f32[8,512]{1,0:T(8,128)S(1)}) custom-call(bf16[512,512]{1,0:T(8,128)(2,1)S(1)} %copy-done.3, f32[512,128]{1,0:T(8,128)S(1)} %pad.4.log_ref, f32[512,512]{1,0:T(8,128)S(1)} %shard_map.114.local_ref, bf16[4,128,128]{2,1,0:T(8,128)(2,1)S(1)} %all-to-all-done.3.enter_ref), custom_call_target="tpu_custom_call" | custom-call | flops 67108864 | bytes 2621440 | tf_op jit(solution)/shard_map/pallas_call | solution.py:32
  105.3 7.8 %all-to-all-start.4 = ((f32[8,1,512]{2,1,0:T(1,128)}), f32[8,1,512]{2,1,0:T(1,128)S(1)}, u32[]{:S(2)}, u32[]{:S(2)}) async-start(f32[8,1,512]{2,1,0:T(1,128)} %copy.23), calls=%async_computation.4 | async-start | bytes 32768 | tf_op jit(solution)/shard_map/all_to_all | solution.py:276
  115.4 5.0 %shard_map.124 = bf16[512,512]{1,0:T(8,128)(2,1)} custom-call(s32[3]{0:T(128)S(1)} %pad_add_fusion.place_ref.refs_0_, s32[256]{0:T(256)S(1)} %copy-done.11, bf16[512,512]{1,0:T(8,128)(2,1)S(1)} %copy-done.10, bf16[512,256]{1,0:T(8,128)(2,1)} %collective-permute-done.3.refs_3_, f32[4,128,512]{2,1,0:T(8,128)S(1)} %copy-done.19, ...), custom_call_target="tpu_custom_call" | custom-call | flops 4000000000 | bytes 3145728 | tf_op jit(solution)/shard_map/pallas_call | solution.py:32
  121.1 1.4 %shard_map.119 = bf16[512,512]{1,0:T(8,128)(2,1)} custom-call(f32[512,512]{1,0:T(8,128)S(1)} %get-tuple-element.21.raw_ref, f32[8,512]{1,0:T(8,128)S(1)} %bitcast.8, bf16[512,512]{1,0:T(8,128)(2,1)S(1)} %copy-done.4, f32[1,512]{1,0:T(1,128)S(1)} %bitcast.10), custom_call_target="tpu_custom_call" | custom-call | flops 2097152 | bytes 2097152 | tf_op jit(solution)/shard_map/pallas_call | solution.py:32
  (57 shorter events, 15.7 us)
Async XLA Ops:
  0.6 1.1 copy-start
  3.6 21.3 %copy-start.2 = (bf16[512,512]{1,0:T(8,128)(2,1)S(1)}, bf16[512,512]{1,0:T(8,128)(2,1)}, u32[]{:S(2)}) copy-start(bf16[512,512]{1,0:T(8,128)(2,1)} %value_ref.3) | copy-start | bytes 1572868
  3.6 21.3 %copy-start.3 = (bf16[512,512]{1,0:T(8,128)(2,1)S(1)}, bf16[512,512]{1,0:T(8,128)(2,1)}, u32[]{:S(2)}) copy-start(bf16[512,512]{1,0:T(8,128)(2,1)} %query_ref.3) | copy-start | bytes 1572868
  5.7 27.0 %collective-permute-start = (bf16[512,256]{1,0:T(8,128)(2,1)}, bf16[512,256]{1,0:T(8,128)(2,1)}, u32[]{:S(2)}, u32[]{:S(2)}) collective-permute-start(bf16[512,256]{1,0:T(8,128)(2,1)} %get-tuple-element.23.refs_3_), channel_id=1, source_target_pairs={{0,32},{8,40},{16,48},{24,56},{32,64},{40,72},{48,80},{56,88},{64,... | collective-permute-start | bytes 786440 | tf_op jit(solution)/shard_map/ppermute | solution.py:366
  14.6 28.4 %collective-permute-start.4 = (bf16[512,256]{1,0:T(8,128)(2,1)}, bf16[512,256]{1,0:T(8,128)(2,1)}, u32[]{:S(2)}, u32[]{:S(2)}) collective-permute-start(bf16[512,256]{1,0:T(8,128)(2,1)} %get-tuple-element.23.refs_3_), channel_id=1, source_target_pairs={{0,8},{8,16},{16,24},{24,32},{32,40},{40,48},{48,56},{56,64},{64,7... | collective-permute-start | bytes 786440 | tf_op jit(solution)/shard_map/ppermute | solution.py:366
  18.1 29.2 %all-to-all-start = ((bf16[4,144,128]{2,1,0:T(8,128)(2,1)}), bf16[4,144,128]{2,1,0:T(8,128)(2,1)S(1)}, u32[]{:S(2)}, u32[]{:S(2)}) async-start(bf16[4,144,128]{2,1,0:T(8,128)(2,1)} %get-tuple-element.20), calls=%async_computation | async-start | bytes 294912 | tf_op jit(solution)/shard_map/all_to_all | solution.py:243
  24.9 1.6 %copy-start.8 = (bf16[512,512]{1,0:T(8,128)(2,1)S(1)}, bf16[512,512]{1,0:T(8,128)(2,1)}, u32[]{:S(2)}) copy-start(bf16[512,512]{1,0:T(8,128)(2,1)} %refs_2_.9) | copy-start | bytes 1572868
  24.9 1.6 %copy-start.11 = (s32[256]{0:T(256)S(1)}, s32[256]{0:T(256)}, u32[]{:S(2)}) copy-start(s32[256]{0:T(256)} %refs_1_.9) | copy-start | bytes 3076
  30.3 26.7 %copy-start.9 = (bf16[512,512]{1,0:T(8,128)(2,1)S(1)}, bf16[512,512]{1,0:T(8,128)(2,1)}, u32[]{:S(2)}) copy-start(bf16[512,512]{1,0:T(8,128)(2,1)} %refs_2_.9) | copy-start | bytes 1572868
  32.7 33.2 %collective-permute-start.1 = (bf16[512,256]{1,0:T(8,128)(2,1)}, bf16[512,256]{1,0:T(8,128)(2,1)}, u32[]{:S(2)}, u32[]{:S(2)}) collective-permute-start(bf16[512,256]{1,0:T(8,128)(2,1)} %collective-permute-done.refs_4_), channel_id=1, source_target_pairs={{0,8},{8,16},{16,24},{24,32},{32,40},{40,48},{48,56},{56,64},{64,7... | collective-permute-start | bytes 786440 | tf_op jit(solution)/shard_map/ppermute | solution.py:366
  43.0 24.9 %collective-permute-start.5 = (bf16[512,256]{1,0:T(8,128)(2,1)}, bf16[512,256]{1,0:T(8,128)(2,1)}, u32[]{:S(2)}, u32[]{:S(2)}) collective-permute-start(bf16[512,256]{1,0:T(8,128)(2,1)} %collective-permute-done.4.refs_3_), channel_id=1, source_target_pairs={{0,8},{8,16},{16,24},{24,32},{32,40},{40,48},{48,56},{56,64},{64,7... | collective-permute-start | bytes 786440 | tf_op jit(solution)/shard_map/ppermute | solution.py:366
  48.0 21.8 %all-to-all-start.1 = ((bf16[4,144,128]{2,1,0:T(8,128)(2,1)}), bf16[4,144,128]{2,1,0:T(8,128)(2,1)S(1)}, u32[]{:S(2)}, u32[]{:S(2)}) async-start(bf16[4,144,128]{2,1,0:T(8,128)(2,1)} %shard_map.115), calls=%async_computation.1 | async-start | bytes 294912 | tf_op jit(solution)/shard_map/all_to_all | solution.py:243
  56.9 1.2 %copy-start.13 = (f32[4,128,512]{2,1,0:T(8,128)S(1)}, f32[4,128,512]{2,1,0:T(8,128)}, u32[]{:S(2)}) copy-start(f32[4,128,512]{2,1,0:T(8,128)} %copy-done.12) | copy-start | bytes 3145732
  65.9 17.7 %collective-permute-start.2 = (bf16[512,256]{1,0:T(8,128)(2,1)}, bf16[512,256]{1,0:T(8,128)(2,1)S(1)}, u32[]{:S(2)}, u32[]{:S(2)}) collective-permute-start(bf16[512,256]{1,0:T(8,128)(2,1)} %collective-permute-done.1.refs_4_), channel_id=1, source_target_pairs={{0,8},{8,16},{16,24},{24,32},{32,40},{40,48},{48,56},{56,64},{64,7... | collective-permute-start | bytes 786440 | tf_op jit(solution)/shard_map/ppermute | solution.py:366
  67.9 26.1 %collective-permute-start.6 = (bf16[512,256]{1,0:T(8,128)(2,1)}, bf16[512,256]{1,0:T(8,128)(2,1)}, u32[]{:S(2)}, u32[]{:S(2)}) collective-permute-start(bf16[512,256]{1,0:T(8,128)(2,1)} %collective-permute-done.5.refs_3_), channel_id=1, source_target_pairs={{0,8},{8,16},{16,24},{24,32},{32,40},{40,48},{48,56},{56,64},{64,7... | collective-permute-start | bytes 786440 | tf_op jit(solution)/shard_map/ppermute | solution.py:366
  70.6 15.0 %all-to-all-start.2 = ((f32[4,136,128]{2,1,0:T(8,128)}), f32[4,136,128]{2,1,0:T(8,128)S(1)}, u32[]{:S(2)}, u32[]{:S(2)}) async-start(f32[4,136,128]{2,1,0:T(8,128)} %shard_map.116), calls=%async_computation.2 | async-start | bytes 557056 | tf_op jit(solution)/shard_map/all_to_all | solution.py:243
  74.8 1.2 copy-start.15
  83.6 29.5 %collective-permute-start.3 = (bf16[512,256]{1,0:T(8,128)(2,1)S(1)}, bf16[512,256]{1,0:T(8,128)(2,1)}, u32[]{:S(2)}, u32[]{:S(2)}) collective-permute-start(bf16[512,256]{1,0:T(8,128)(2,1)S(1)} %collective-permute-done.2.refs_4_), channel_id=1, source_target_pairs={{0,8},{8,16},{16,24},{24,32},{32,40},{40,48},{48,56},{56,64},{64,7... | collective-permute-start | bytes 786440 | tf_op jit(solution)/shard_map/ppermute | solution.py:366
  86.9 16.1 %all-to-all-start.3 = ((bf16[4,128,128]{2,1,0:T(8,128)(2,1)}), bf16[4,128,128]{2,1,0:T(8,128)(2,1)S(1)}, u32[]{:S(2)}, u32[]{:S(2)}) async-start(bf16[4,128,128]{2,1,0:T(8,128)(2,1)} %shard_map.117), calls=%async_computation.3 | async-start | bytes 262144 | tf_op jit(solution)/shard_map/all_to_all | solution.py:243
  93.9 1.2 %copy-start.17 = (f32[4,128,512]{2,1,0:T(8,128)S(1)}, f32[4,128,512]{2,1,0:T(8,128)}, u32[]{:S(2)}) copy-start(f32[4,128,512]{2,1,0:T(8,128)} %copy-done.16) | copy-start | bytes 3145732
  105.3 15.2 %all-to-all-start.4 = ((f32[8,1,512]{2,1,0:T(1,128)}), f32[8,1,512]{2,1,0:T(1,128)S(1)}, u32[]{:S(2)}, u32[]{:S(2)}) async-start(f32[8,1,512]{2,1,0:T(1,128)} %copy.23), calls=%async_computation.4 | async-start | bytes 32768 | tf_op jit(solution)/shard_map/all_to_all | solution.py:276
  113.1 1.0 copy-start.10
  114.1 1.2 copy-start.19
  115.4 5.1 %copy-start.4 = (bf16[512,512]{1,0:T(8,128)(2,1)S(1)}, bf16[512,512]{1,0:T(8,128)(2,1)}, u32[]{:S(2)}) copy-start(bf16[512,512]{1,0:T(8,128)(2,1)} %gate_ref.1) | copy-start | bytes 1572868
  (8 other events, 7.6 us)

commit v3 on v2

--- a/solution.py
+++ b/solution.py
@@ -17,18 +17,20 @@
 NEG = -1e30
 LOG_FLOOR = -1000.0
 LOG_ROWS = 16
-QUAD = 4
+SAME = 8
+LINE = 16
 F32 = jnp.float32
 BF16 = jnp.bfloat16
 VMEM_LIMIT = 48 * 1024 * 1024
 COST = 4 * 10**9
 
 
-def call(body, outs, operands, *, flops, moved, exps=0, scratch=(), smem=(), aliases=None):
-    specs = [
-        pl.BlockSpec(memory_space=pltpu.SMEM if i in smem else pltpu.VMEM)
-        for i in range(len(operands))
-    ]
+def call(
+    body, outs, operands, *, flops, moved, exps=0, scratch=(), smem=(), aliases=None, after=()
+):
+    operands = (*operands, *after)
+    spaces = [pltpu.SMEM if i in smem else pltpu.VMEM for i in range(len(operands) - len(after))]
+    specs = [pl.BlockSpec(memory_space=m) for m in spaces + [pl.ANY] * len(after)]
     return pl.pallas_call(
         body,
         out_shape=outs,
@@ -55,12 +57,19 @@
 
 
 def block_sums(log_ref):
+    return [dot(tri, logs, ((1,), (1,)), lax.Precision.HIGHEST) for tri, logs in blocks_of(log_ref)]
+
+
+def block_sums_across(log_ref):
+    return [dot(logs, tri, ((1,), (1,)), lax.Precision.HIGHEST) for tri, logs in blocks_of(log_ref)]
+
+
+def blocks_of(log_ref):
     rows = lax.broadcasted_iota(jnp.int32, (BLK, BLK), 0)
     cols = lax.broadcasted_iota(jnp.int32, (BLK, BLK), 1)
     tri = (rows >= cols).astype(F32)
     return [
-        dot(tri, log_ref[b * BLK : (b + 1) * BLK, :], ((1,), (0,)), lax.Precision.HIGHEST)
-        for b in range(log_ref.shape[0] // BLK)
+        (tri, log_ref[:, b * BLK : (b + 1) * BLK]) for b in range(log_ref.shape[1] // BLK)
     ]
 
 
@@ -96,15 +105,17 @@
             else:
                 state = jnp.exp(end) * state + local
             total = total + end
-        send_ref[h, :HD, :] = state.astype(BF16)
         total = jnp.broadcast_to(jnp.maximum(total, LOG_FLOOR), (1, HD))
-        send_ref[h, HD:, :] = log_rows(total)
+        share, size = send_ref.shape[0] // heads, send_ref.shape[1] - LOG_ROWS
+        for j in range(share):
+            send_ref[h * share + j, :size, :] = state[j * size : (j + 1) * size].astype(BF16)
+            send_ref[h * share + j, size:, :] = log_rows(total)
 
 
 def local_body(query_ref, key_ref, value_ref, log_ref, first_ref, raw_ref):
     heads = key_ref.shape[1] // HD
     sums = block_sums(log_ref)
-    across = [s.T for s in sums]
+    across = block_sums_across(log_ref)
     rows_i = lax.broadcasted_iota(jnp.int32, (BLK, BLK), 0)
     cols_i = lax.broadcasted_iota(jnp.int32, (BLK, BLK), 1)
     causal = rows_i >= cols_i
@@ -126,10 +137,6 @@
             raw_ref[rows, lanes] = raw
 
 
-def log_of(block):
-    return jnp.sum(block[HD:, :].astype(F32), axis=0, keepdims=True)
-
-
 def fold(parts):
     state, total = parts[0]
     for s, l in parts[1:]:
@@ -138,44 +145,37 @@
     return state, jnp.maximum(total, LOG_FLOOR)
 
 
-def parts_of(got_ref):
+def parts_of(got_ref, size):
     return [
-        (got_ref[j, :HD, :].astype(F32), log_of(got_ref[j])) for j in range(got_ref.shape[0])
+        (
+            got_ref[j, :size, :].astype(F32),
+            jnp.sum(got_ref[j, size:, :].astype(F32), axis=0, keepdims=True),
+        )
+        for j in range(got_ref.shape[0])
     ]
 
 
-def group_body(got_ref, send_ref):
-    state, total = fold(parts_of(got_ref))
-    state = state.astype(send_ref.dtype)
-    rows = log_rows(total)
-    if send_ref.dtype == F32:
-        row = lax.broadcasted_iota(jnp.int32, (send_ref.shape[1] - HD, HD), 0)
-        rows = jnp.where(row == 0, total, 0.0)
+def line_body(got_ref, send_ref):
+    size = got_ref.shape[1] - LOG_ROWS
+    state, total = fold(parts_of(got_ref, size))
+    row = lax.broadcasted_iota(jnp.int32, (send_ref.shape[1] - size, HD), 0)
+    rows = jnp.where(row == 0, total, 0.0)
     for j in range(send_ref.shape[0]):
-        send_ref[j, :HD, :] = state
-        send_ref[j, HD:, :] = rows
+        send_ref[j, :size, :] = state
+        send_ref[j, size:, :] = rows
 
 
 def before(parts, place):
-    state = jnp.zeros((HD, HD), F32)
+    state = jnp.zeros_like(parts[0][0])
     for j, (s, l) in enumerate(parts[:-1]):
         state = jnp.where(j < place, jnp.exp(l) * state + s, state)
     return state
 
 
-def log_before(parts, place):
-    total = jnp.zeros((1, HD), F32)
-    for j, (_, l) in enumerate(parts[:-1]):
-        total = jnp.where(j < place, total + l, total)
-    return total
-
-
-def enter_body(place_ref, mine_ref, line_ref, wide_ref, send_ref):
-    line = parts_of(line_ref)
-    wide = parts_of(wide_ref)
-    state = before(wide, place_ref[1])
-    entering = jnp.exp(log_before(line, place_ref[0])) * state + before(line, place_ref[0])
-    for j, (s, l) in enumerate(parts_of(mine_ref)):
+def enter_body(place_ref, line_ref, wide_ref, send_ref):
+    size = send_ref.shape[1]
+    entering = before(parts_of(wide_ref, size), place_ref[0])
+    for j, (s, l) in enumerate(parts_of(line_ref, size)):
         send_ref[j] = entering.astype(BF16)
         entering = jnp.exp(l) * entering + s
 
@@ -183,7 +183,7 @@
 def raw_body(query_ref, log_ref, local_ref, enter_ref, raw_ref, square_ref):
     heads = query_ref.shape[1] // HD
     sums = block_sums(log_ref)
-    ahead = jnp.zeros((1, HD), F32)
+    ahead = jnp.zeros((1, heads), F32)
     for b, cum in enumerate(sums):
         rows = slice(b * BLK, (b + 1) * BLK)
         for h in range(heads):
@@ -198,7 +198,7 @@
 
 
 def norm_body(columns, raw_ref, square_ref, gate_ref, gain_ref, out_ref):
-    ones = jnp.ones((square_ref.shape[0], HD), F32)
+    ones = jnp.full((square_ref.shape[0], HD), 1.0 / SAME, F32)
     total = dot(square_ref[...], ones, ((0,), (0,)), lax.Precision.HIGHEST)
     scale = lax.rsqrt(total / columns + EPS)
     for h in range(raw_ref.shape[1] // HD):
@@ -210,11 +210,11 @@
 def states(lin_key, lin_value, log_decay, soft_key, soft_value):
     tokens, features = lin_key.shape
     heads = features // HD
-    logs = jnp.pad(log_decay, ((0, 0), (0, HD - heads)))
+    logs = log_decay.T
     send, first, moving = call(
         states_body,
         (
-            jax.ShapeDtypeStruct((heads, HD + LOG_ROWS, HD), BF16),
+            jax.ShapeDtypeStruct((LINE, heads * HD // LINE + LOG_ROWS, HD), BF16),
             jax.ShapeDtypeStruct((heads, HD, HD), F32),
             jax.ShapeDtypeStruct((tokens, 2 * soft_key.shape[1]), BF16),
         ),
@@ -225,24 +225,18 @@
     return logs, send, first, moving
 
 
-def lightning(lin_query, lin_key, lin_value, lin_gate, logs, send, first, norm_gain, place):
+def lightning_local(lin_query, lin_key, lin_value, logs, send, first):
     tokens, features = lin_query.shape
     heads = features // HD
     shards = lax.axis_size("seq")
     peers = lax.axis_size("head")
-    near = [[QUAD * g + j for j in range(QUAD)] for g in range(shards // QUAD)]
-    span = QUAD * QUAD
-    line = [
-        [span * x + QUAD * a + b for a in range(QUAD)]
-        for x in range(shards // span)
-        for b in range(QUAD)
-    ]
-    wide = [[span * x + r for x in range(shards // span)] for r in range(span)]
+    line = [[LINE * x + z for z in range(LINE)] for x in range(shards // LINE)]
+    wide = [[LINE * x + z for x in range(shards // LINE)] for z in range(LINE)]
 
     def swap(array, groups):
         return lax.all_to_all(array, "seq", 0, 0, axis_index_groups=groups, tiled=True)
 
-    mine = swap(send, near)
+    lines = swap(send, line)
     local = call(
         local_body,
         jax.ShapeDtypeStruct((tokens, features), F32),
@@ -251,23 +245,31 @@
         moved=10 * tokens * features,
     )
     small = dict(flops=10 * heads * HD * HD, moved=4 * heads * HD * HD)
-    sent = jax.ShapeDtypeStruct((QUAD, HD + LOG_ROWS, HD), BF16)
-    exact = jax.ShapeDtypeStruct((shards // span, HD + 8, HD), F32)
-    lines = swap(call(group_body, sent, (mine,), **small), line)
-    wides = swap(call(group_body, exact, (lines,), **small), wide)
+    size = heads * HD // LINE
+    total = jax.ShapeDtypeStruct((shards // LINE, size + 8, HD), F32)
+    total = call(line_body, total, (lines,), **small)
+    return local, lines, total, swap, line, wide, small
+
+
+def lightning(lin_query, lin_gate, logs, norm_gain, place, local, lines, total, swap, line, wide, small):
+    tokens, features = lin_query.shape
+    heads = features // HD
+    peers = lax.axis_size("head")
+    size = heads * HD // LINE
+    wides = swap(total, wide)
     entering = call(
         enter_body,
-        jax.ShapeDtypeStruct((heads, HD, HD), BF16),
-        (place, mine, lines, wides),
+        jax.ShapeDtypeStruct((LINE, size, HD), BF16),
+        (place, lines, wides),
         smem=(0,),
         **small,
     )
-    entering = swap(entering, near)
+    entering = swap(entering, line).reshape(heads, HD, HD)
     raw, squares = call(
         raw_body,
         (
             jax.ShapeDtypeStruct((tokens, features), F32),
-            jax.ShapeDtypeStruct((peers, tokens), F32),
+            jax.ShapeDtypeStruct((peers * SAME, tokens), F32),
         ),
         (lin_query, logs, local, entering),
         flops=2 * tokens * features * HD,
@@ -288,15 +290,16 @@
 
 
 def attend_body(backs, opening, final, *refs):
-    refs = list(refs)
-    place_ref, docs_ref, query_ref = refs[:3]
-    pieces = refs[3 : 3 + len(backs)]
-    rest = refs[3 + len(backs) :]
+    place_ref, docs_ref, query_ref, piece_ref = refs[:4]
+    pieces = [
+        piece_ref.at[:, 2 * HD * j : 2 * HD * (j + 1)] for j in range(piece_ref.shape[1] // (2 * HD))
+    ]
+    rest = refs[4:]
     tokens, features = query_ref.shape
     heads = features // HD
     blocks = tokens // MBLK
     rows = heads * MBLK
-    shard = place_ref[2]
+    shard = place_ref[1]
     if opening:
         acc_ref, top_ref, sum_ref = rest
     elif final:
@@ -361,48 +364,59 @@
                 ].astype(BF16)
 
 
+def join_body(first_ref, second_ref, *rest):
+    both_ref = rest[-1]
+    both_ref[:, : first_ref.shape[1]] = first_ref[...]
+    both_ref[:, first_ref.shape[1] :] = second_ref[...]
+
+
 def forward(array, steps):
     shards = lax.axis_size("seq")
     return lax.ppermute(array, "seq", [(s, s + steps) for s in range(shards - steps)])
 
 
-def attend(soft_query, own, doc_ids, place):
+def attend(soft_query, own, doc_ids, place, after):
     tokens, features = soft_query.shape
     blocks = tokens // MBLK
     hops = (DOC_MOST + blocks - 2) // blocks
     heads = features // HD
     half = (hops + 1) // 2
-    pieces = {0: own, half: forward(own, half)}
-    for back in range(1, half):
-        pieces[back] = forward(pieces[back - 1], 1)
-    for back in range(half + 1, hops + 1):
-        pieces[back] = forward(pieces[back - 1], 1)
     rows = heads * MBLK
     carry = (
         jax.ShapeDtypeStruct((blocks, HD, rows), F32),
         jax.ShapeDtypeStruct((blocks, 1, rows), F32),
         jax.ShapeDtypeStruct((blocks, 1, rows), F32),
     )
-    calls = [(0,)] + [(b, b + half - 1) for b in range(1, half)]
-    calls.append(tuple(range(2 * half - 1, hops + 1)))
-    state = ()
-    for backs in calls:
-        opening, final = backs == calls[0], backs == calls[-1]
-        operands = (place, doc_ids, soft_query, *(pieces[b] for b in backs), *state)
-        aliases = None
-        if not opening and not final:
-            aliases = {len(operands) - 3 + j: j for j in range(3)}
-        state = call(
-            functools.partial(attend_body, backs, opening, final),
+
+    def absorb(state, backs, array, final=False):
+        operands = (place, doc_ids, soft_query, array, *state)
+        aliases = {len(operands) - 3 + j: j for j in range(3)}
+        return call(
+            functools.partial(attend_body, backs, not state, final),
             jax.ShapeDtypeStruct((tokens, features), BF16) if final else carry,
             operands,
             smem=(0, 1),
-            aliases=aliases,
+            aliases=aliases if state and not final else None,
             scratch=tuple(pltpu.VMEM(c.shape, c.dtype) for c in carry) if final else (),
             flops=len(backs) * COST,
             moved=12 * tokens * features,
             exps=len(backs) * heads * tokens * tokens,
         )
+
+    far = forward(own, half)
+    state = absorb((), (0,), own)
+    moving = call(
+        join_body,
+        jax.ShapeDtypeStruct((tokens, 2 * own.shape[1]), BF16),
+        (own, far),
+        flops=0,
+        moved=4 * own.size,
+        after=(state[1], *after),
+    )
+    state = absorb(state, (half,), far)
+    for back in range(1, half):
+        moving = forward(moving, 1)
+        state = absorb(state, (back, back + half), moving, back == half - 1)
     return state
 
 
@@ -419,13 +433,11 @@
     doc_ids,
 ):
     shard = lax.axis_index("seq")
-    span = QUAD * QUAD
-    place = jnp.stack([(shard % span) // QUAD, shard // span, shard]).astype(jnp.int32)
+    place = jnp.stack([shard // LINE, shard]).astype(jnp.int32)
     logs, send, first, moving = states(lin_key, lin_value, log_decay, soft_key, soft_value)
-    soft_out = attend(soft_query, moving, doc_ids, place)
-    lin_out = lightning(
-        lin_query, lin_key, lin_value, lin_gate, logs, send, first, norm_gain, place
-    )
+    parts = lightning_local(lin_query, lin_key, lin_value, logs, send, first)
+    soft_out = attend(soft_query, moving, doc_ids, place, (parts[0], parts[2]))
+    lin_out = lightning(lin_query, lin_gate, logs, norm_gain, place, *parts)
     return (lin_out, soft_out)
 
 

time: 124 us -> 130 us (1.048)
  the two profiles are of different devices: /device:TPU:45 before, /device:TPU:10 now
where the time goes in v3:
time: 130 us; the launch traced here: 129 us
  starting transfers between devices  57.1 us (44%)
  waiting for transfers between devices  30.3 us (23%)
  Pallas kernels  28.7 us (22%)
  local copies, waits for them, and re-layouts  11.8 us (9%)
    all_to_all x3, starting transfers between devices, swap(): lax.all_to_all(array, 'seq', 0, 0, axis_index_groups=groups, tiled=True)  37.7 us
    pallas_call x12, Pallas kernels, call(): pl.pallas_call(body, out_shape=outs, in_specs=specs, out_specs=jax.tree.m...  28.7 us
    all_to_all x3, waiting for transfers between devices, swap(): lax.all_to_all(array, 'seq', 0, 0, axis_index_groups=groups, tiled=True)  15.3 us
    ppermute x4, waiting for transfers between devices, forward(): lax.ppermute(array, 'seq', [(s, s + steps) for s in range(shards - steps)])  15 us
    ppermute x4, starting transfers between devices, forward(): lax.ppermute(array, 'seq', [(s, s + steps) for s in range(shards - steps)])  14.5 us
    unnamed x44, local copies, waits for them, and re-layouts  11.8 us
    all_to_all x1, starting transfers between devices, lightning(): squares = lax.all_to_all(squares, 'head', 0, 0, tiled=True)  4.92 us
  transfers between devices with their start and end apart: 8, of which 4 were waited for; matrix products, arithmetic and copies ran while one was open for 0% of the time, Pallas kernels for 17%

profile of v3, /device:TPU:10, one launch (start us, length us, event | category | flops | bytes accessed | tf_op | source)
XLA Modules:
  0.0 128.8 jit_solution(4931297821795079327)
XLA Ops:
  5.2 2.2 %shard_map.113 = (bf16[16,48,128]{2,1,0:T(8,128)(2,1)}, f32[4,128,128]{2,1,0:T(8,128)S(1)}, bf16[512,256]{1,0:T(8,128)(2,1)S(1)}) custom-call(bf16[512,512]{1,0:T(8,128)(2,1)S(1)} %copy-done, bf16[512,512]{1,0:T(8,128)(2,1)S(1)} %copy-done.2, f32[4,512]{1,0:T(4,128)S(1)} %bitcast.9, bf16[512,128]{1,0:T(8,128)(2,1)S(1)} %copy-done.6, ...), custom_call_target="tpu_custom_call" | custom-call | flops 134217728 | bytes 1048576 | tf_op jit(solution)/shard_map/pallas_call | solution.py:34
  7.4 15.3 %all-to-all-start = ((bf16[16,48,128]{2,1,0:T(8,128)(2,1)}), bf16[16,48,128]{2,1,0:T(8,128)(2,1)S(1)}, u32[]{:S(2)}, u32[]{:S(2)}) async-start(bf16[16,48,128]{2,1,0:T(8,128)(2,1)} %get-tuple-element.20), calls=%async_computation | async-start | bytes 393216 | tf_op jit(solution)/shard_map/all_to_all | solution.py:237
  22.7 7.7 %collective-permute-start = (bf16[512,256]{1,0:T(8,128)(2,1)S(1)}, bf16[512,256]{1,0:T(8,128)(2,1)S(1)}, u32[]{:S(2)}, u32[]{:S(2)}) collective-permute-start(bf16[512,256]{1,0:T(8,128)(2,1)S(1)} %get-tuple-element.23.refs_3_.first_ref), channel_id=1, source_target_pairs={{0,32},{8,40},{16,48},{24,56},{32,64},{40,72},{48,80},{56,88},{64,... | collective-permute-start | bytes 786440 | tf_op jit(solution)/shard_map/ppermute | solution.py:375
  30.5 10.5 %all-to-all-done.got_ref.line_ref = bf16[16,48,128]{2,1,0:T(8,128)(2,1)S(1)} async-done(((bf16[16,48,128]{2,1,0:T(8,128)(2,1)}), bf16[16,48,128]{2,1,0:T(8,128)(2,1)S(1)}, u32[]{:S(2)}, u32[]{:S(2)}) %all-to-all-start) | async-done | bytes 196640 | tf_op jit(solution)/shard_map/all_to_all | solution.py:237
  41.8 5.0 %all-to-all-start.1 = ((f32[4,40,128]{2,1,0:T(8,128)}), f32[4,40,128]{2,1,0:T(8,128)S(1)}, u32[]{:S(2)}, u32[]{:S(2)}) async-start(f32[4,40,128]{2,1,0:T(8,128)} %shard_map.115.rest_2_), calls=%async_computation.1 | async-start | bytes 163840 | tf_op jit(solution)/shard_map/all_to_all | solution.py:237
  46.8 2.4 %shard_map.119 = (f32[4,128,512]{2,1,0:T(8,128)S(1)}, f32[4,1,512]{2,1,0:T(1,128)S(1)}, f32[4,1,512]{2,1,0:T(1,128)S(1)}) custom-call(s32[2]{0:T(128)S(1)} %pad_add_fusion.place_ref.refs_0_, s32[256]{0:T(256)S(1)} %copy-done.15, bf16[512,512]{1,0:T(8,128)(2,1)S(1)} %copy-done.11, bf16[512,256]{1,0:T(8,128)(2,1)S(1)} %get-tuple-element.23.refs_3_.first_ref), custom_call_target="tpu_custom_call" | custom-call | flops 4000000000 | bytes 3145728 | tf_op jit(solution)/shard_map/pallas_call | solution.py:34
  49.2 2.0 %shard_map.114.local_ref.rest_1_ = f32[512,512]{1,0:T(8,128)S(1)} custom-call(bf16[512,512]{1,0:T(8,128)(2,1)S(1)} %copy-done.4, bf16[512,512]{1,0:T(8,128)(2,1)S(1)} %copy-done.1, bf16[512,512]{1,0:T(8,128)(2,1)S(1)} %copy-done.3, f32[4,512]{1,0:T(4,128)S(1)} %bitcast.10, f32[4,128,128]{2,1,0:T(8,128)S(1)} %get-tuple-element.19.first_ref), custom_call_target="tpu_custom_call" | custom-call | flops 268435456 | bytes 2621440 | tf_op jit(solution)/shard_map/pallas_call | solution.py:34
  51.2 2.9 %collective-permute-done.second_ref.refs_3_ = bf16[512,256]{1,0:T(8,128)(2,1)S(1)} collective-permute-done((bf16[512,256]{1,0:T(8,128)(2,1)S(1)}, bf16[512,256]{1,0:T(8,128)(2,1)S(1)}, u32[]{:S(2)}, u32[]{:S(2)}) %collective-permute-start) | collective-permute-done | bytes 262176 | tf_op jit(solution)/shard_map/ppermute | solution.py:375
  54.2 2.9 %collective-permute-start.1 = (bf16[512,512]{1,0:T(8,128)(2,1)S(1)}, bf16[512,512]{1,0:T(8,128)(2,1)}, u32[]{:S(2)}, u32[]{:S(2)}) collective-permute-start(bf16[512,512]{1,0:T(8,128)(2,1)S(1)} %shard_map.120), channel_id=1, source_target_pairs={{0,8},{8,16},{16,24},{24,32},{32,40},{40,48},{48,56},{56,64},{64,7... | collective-permute-start | bytes 1572872 | tf_op jit(solution)/shard_map/ppermute | solution.py:375
  57.1 1.3 shard_map.116
  58.4 17.4 %all-to-all-start.2 = ((bf16[16,32,128]{2,1,0:T(8,128)(2,1)}), bf16[16,32,128]{2,1,0:T(8,128)(2,1)S(1)}, u32[]{:S(2)}, u32[]{:S(2)}) async-start(bf16[16,32,128]{2,1,0:T(8,128)(2,1)} %shard_map.116), calls=%async_computation.2 | async-start | bytes 262144 | tf_op jit(solution)/shard_map/all_to_all | solution.py:237
  76.8 1.2 copy-done.17
  78.1 3.3 %shard_map.121 = (f32[4,128,512]{2,1,0:T(8,128)S(1)}, f32[4,1,512]{2,1,0:T(1,128)S(1)}, f32[4,1,512]{2,1,0:T(1,128)S(1)}) custom-call(s32[2]{0:T(128)S(1)} %pad_add_fusion.place_ref.refs_0_, s32[256]{0:T(256)S(1)} %copy-done.15, bf16[512,512]{1,0:T(8,128)(2,1)S(1)} %copy-done.12, ...), custom_call_target="tpu_custom_call", output_to_operand_aliasing={{0}: (4, {}), {1}: (5, {}), {2}: (6, {})} | custom-call | flops 4000000000 | bytes 3145728 | tf_op jit(solution)/shard_map/pallas_call | solution.py:34
  82.4 1.9 %collective-permute-start.2 = (bf16[512,512]{1,0:T(8,128)(2,1)}, bf16[512,512]{1,0:T(8,128)(2,1)}, u32[]{:S(2)}, u32[]{:S(2)}) collective-permute-start(bf16[512,512]{1,0:T(8,128)(2,1)} %collective-permute-done.1.refs_3_), channel_id=1, source_target_pairs={{0,8},{8,16},{16,24},{24,32},{32,40},{40,48},{48,56},{56,64},{64,7... | collective-permute-start | bytes 1572872 | tf_op jit(solution)/shard_map/ppermute | solution.py:375
  84.3 4.8 %all-to-all-done.2 = bf16[16,32,128]{2,1,0:T(8,128)(2,1)S(1)} async-done(((bf16[16,32,128]{2,1,0:T(8,128)(2,1)}), bf16[16,32,128]{2,1,0:T(8,128)(2,1)S(1)}, u32[]{:S(2)}, u32[]{:S(2)}) %all-to-all-start.2) | async-done | bytes 131104 | tf_op jit(solution)/shard_map/all_to_all | solution.py:237
  89.1 2.5 %shard_map.117 = (f32[512,512]{1,0:T(8,128)S(1)}, f32[64,512]{1,0:T(8,128)}) custom-call(bf16[512,512]{1,0:T(8,128)(2,1)S(1)} %copy-done.4, f32[4,512]{1,0:T(4,128)S(1)} %bitcast.11, f32[512,512]{1,0:T(8,128)S(1)} %shard_map.114.local_ref.rest_1_, bf16[4,128,128]{2,1,0:T(8,128)(2,1)S(1)} %bitcast.8), custom_call_target="tpu_custom_call" | custom-call | flops 67108864 | bytes 2621440 | tf_op jit(solution)/shard_map/pallas_call | solution.py:34
  91.5 4.9 %all-to-all-start.3 = ((f32[8,8,512]{2,1,0:T(8,128)}), f32[8,8,512]{2,1,0:T(8,128)S(1)}, u32[]{:S(2)}, u32[]{:S(2)}) async-start(f32[8,8,512]{2,1,0:T(8,128)} %bitcast.4), calls=%async_computation.3 | async-start | bytes 262144 | tf_op jit(solution)/shard_map/all_to_all | solution.py:278
  97.5 1.2 copy-done.19
  98.7 4.2 %shard_map.122 = (f32[4,128,512]{2,1,0:T(8,128)S(1)}, f32[4,1,512]{2,1,0:T(1,128)S(1)}, f32[4,1,512]{2,1,0:T(1,128)S(1)}) custom-call(s32[2]{0:T(128)S(1)} %pad_add_fusion.place_ref.refs_0_, s32[256]{0:T(256)S(1)} %copy-done.15, bf16[512,512]{1,0:T(8,128)(2,1)S(1)} %copy-done.13, ...), custom_call_target="tpu_custom_call", output_to_operand_aliasing={{0}: (4, {}), {1}: (5, {}), {2}: (6, {})} | custom-call | flops 8000000000 | bytes 3145728 | tf_op jit(solution)/shard_map/pallas_call | solution.py:34
  104.6 1.4 %shard_map.118 = bf16[512,512]{1,0:T(8,128)(2,1)} custom-call(f32[512,512]{1,0:T(8,128)S(1)} %get-tuple-element.21.raw_ref, f32[64,512]{1,0:T(8,128)S(1)} %bitcast.7, bf16[512,512]{1,0:T(8,128)(2,1)S(1)} %copy-done.5, f32[1,512]{1,0:T(1,128)S(1)} %bitcast.12), custom_call_target="tpu_custom_call" | custom-call | flops 2097152 | bytes 2097152 | tf_op jit(solution)/shard_map/pallas_call | solution.py:34
  106.0 1.9 %collective-permute-start.3 = (bf16[512,512]{1,0:T(8,128)(2,1)}, bf16[512,512]{1,0:T(8,128)(2,1)S(1)}, u32[]{:S(2)}, u32[]{:S(2)}) collective-permute-start(bf16[512,512]{1,0:T(8,128)(2,1)} %collective-permute-done.2.refs_3_), channel_id=1, source_target_pairs={{0,8},{8,16},{16,24},{24,32},{32,40},{40,48},{48,56},{56,64},{64,7... | collective-permute-start | bytes 1572872 | tf_op jit(solution)/shard_map/ppermute | solution.py:375
  107.9 4.2 %shard_map.123 = (f32[4,128,512]{2,1,0:T(8,128)S(1)}, f32[4,1,512]{2,1,0:T(1,128)S(1)}, f32[4,1,512]{2,1,0:T(1,128)S(1)}) custom-call(s32[2]{0:T(128)S(1)} %pad_add_fusion.place_ref.refs_0_, s32[256]{0:T(256)S(1)} %copy-done.15, bf16[512,512]{1,0:T(8,128)(2,1)S(1)} %copy-done.14, ...), custom_call_target="tpu_custom_call", output_to_operand_aliasing={{0}: (4, {}), {1}: (5, {}), {2}: (6, {})} | custom-call | flops 8000000000 | bytes 3145728 | tf_op jit(solution)/shard_map/pallas_call | solution.py:34
  112.1 12.1 %collective-permute-done.3.refs_3_ = bf16[512,512]{1,0:T(8,128)(2,1)S(1)} collective-permute-done((bf16[512,512]{1,0:T(8,128)(2,1)}, bf16[512,512]{1,0:T(8,128)(2,1)S(1)}, u32[]{:S(2)}, u32[]{:S(2)}) %collective-permute-start.3) | collective-permute-done | bytes 524320 | tf_op jit(solution)/shard_map/ppermute | solution.py:375
  124.2 4.7 %shard_map.124 = bf16[512,512]{1,0:T(8,128)(2,1)} custom-call(s32[2]{0:T(128)S(1)} %pad_add_fusion.place_ref.refs_0_, s32[256]{0:T(256)S(1)} %copy-done.15, bf16[512,512]{1,0:T(8,128)(2,1)S(1)} %copy-done.14, bf16[512,512]{1,0:T(8,128)(2,1)S(1)} %collective-permute-done.3.refs_3_, f32[4,128,512]{2,1,0:T(8,128)S(1)} %get-tuple-element.33.refs_4_, ...), custom_call_target="tpu_custom_call" | custom-call | flops 8000000000 | bytes 3145728 | tf_op jit(solution)/shard_map/pallas_call | solution.py:34
  (49 shorter events, 10.1 us)
Async XLA Ops:
  0.6 1.0 copy-start
  1.7 1.0 copy-start.2
  7.4 39.4 %copy-start.11 = (bf16[512,512]{1,0:T(8,128)(2,1)S(1)}, bf16[512,512]{1,0:T(8,128)(2,1)}, u32[]{:S(2)}) copy-start(bf16[512,512]{1,0:T(8,128)(2,1)} %refs_2_.9) | copy-start | bytes 1572868
  7.4 33.7 %all-to-all-start = ((bf16[16,48,128]{2,1,0:T(8,128)(2,1)}), bf16[16,48,128]{2,1,0:T(8,128)(2,1)S(1)}, u32[]{:S(2)}, u32[]{:S(2)}) async-start(bf16[16,48,128]{2,1,0:T(8,128)(2,1)} %get-tuple-element.20), calls=%async_computation | async-start | bytes 393216 | tf_op jit(solution)/shard_map/all_to_all | solution.py:237
  22.7 31.4 %collective-permute-start = (bf16[512,256]{1,0:T(8,128)(2,1)S(1)}, bf16[512,256]{1,0:T(8,128)(2,1)S(1)}, u32[]{:S(2)}, u32[]{:S(2)}) collective-permute-start(bf16[512,256]{1,0:T(8,128)(2,1)S(1)} %get-tuple-element.23.refs_3_.first_ref), channel_id=1, source_target_pairs={{0,32},{8,40},{16,48},{24,56},{32,64},{40,72},{48,80},{56,88},{64,... | collective-permute-start | bytes 786440 | tf_op jit(solution)/shard_map/ppermute | solution.py:375
  41.8 5.0 %copy-start.15 = (s32[256]{0:T(256)S(1)}, s32[256]{0:T(256)}, u32[]{:S(2)}) copy-start(s32[256]{0:T(256)} %refs_1_.9) | copy-start | bytes 3076
  41.8 15.3 %all-to-all-start.1 = ((f32[4,40,128]{2,1,0:T(8,128)}), f32[4,40,128]{2,1,0:T(8,128)S(1)}, u32[]{:S(2)}, u32[]{:S(2)}) async-start(f32[4,40,128]{2,1,0:T(8,128)} %shard_map.115.rest_2_), calls=%async_computation.1 | async-start | bytes 163840 | tf_op jit(solution)/shard_map/all_to_all | solution.py:237
  46.7 2.4 %copy-start.1 = (bf16[512,512]{1,0:T(8,128)(2,1)S(1)}, bf16[512,512]{1,0:T(8,128)(2,1)}, u32[]{:S(2)}) copy-start(bf16[512,512]{1,0:T(8,128)(2,1)} %key_ref.3) | copy-start | bytes 1572868
  46.8 2.4 %copy-start.3 = (bf16[512,512]{1,0:T(8,128)(2,1)S(1)}, bf16[512,512]{1,0:T(8,128)(2,1)}, u32[]{:S(2)}) copy-start(bf16[512,512]{1,0:T(8,128)(2,1)} %value_ref.3) | copy-start | bytes 1572868
  46.8 2.4 %copy-start.4 = (bf16[512,512]{1,0:T(8,128)(2,1)S(1)}, bf16[512,512]{1,0:T(8,128)(2,1)}, u32[]{:S(2)}) copy-start(bf16[512,512]{1,0:T(8,128)(2,1)} %query_ref.3) | copy-start | bytes 1572868
  46.8 2.4 %copy-start.9 = (f32[512,4]{0,1:T(4,128)S(1)}, f32[512,4]{0,1:T(4,128)}, u32[]{:S(2)}) copy-start(f32[512,4]{0,1:T(4,128)} %param.14) | copy-start | bytes 24580
  49.2 2.0 %copy-start.16 = (f32[4,128,512]{2,1,0:T(8,128)}, f32[4,128,512]{2,1,0:T(8,128)S(1)}, u32[]{:S(2)}) copy-start(f32[4,128,512]{2,1,0:T(8,128)S(1)} %get-tuple-element.25.refs_4_) | copy-start | bytes 3145732
  54.2 28.2 %collective-permute-start.1 = (bf16[512,512]{1,0:T(8,128)(2,1)S(1)}, bf16[512,512]{1,0:T(8,128)(2,1)}, u32[]{:S(2)}, u32[]{:S(2)}) collective-permute-start(bf16[512,512]{1,0:T(8,128)(2,1)S(1)} %shard_map.120), channel_id=1, source_target_pairs={{0,8},{8,16},{16,24},{24,32},{32,40},{40,48},{48,56},{56,64},{64,7... | collective-permute-start | bytes 1572872 | tf_op jit(solution)/shard_map/ppermute | solution.py:375
  58.4 30.7 %all-to-all-start.2 = ((bf16[16,32,128]{2,1,0:T(8,128)(2,1)}), bf16[16,32,128]{2,1,0:T(8,128)(2,1)S(1)}, u32[]{:S(2)}, u32[]{:S(2)}) async-start(bf16[16,32,128]{2,1,0:T(8,128)(2,1)} %shard_map.116), calls=%async_computation.2 | async-start | bytes 262144 | tf_op jit(solution)/shard_map/all_to_all | solution.py:237
  75.8 1.0 copy-start.12
  76.8 1.2 copy-start.17
  82.4 23.6 %collective-permute-start.2 = (bf16[512,512]{1,0:T(8,128)(2,1)}, bf16[512,512]{1,0:T(8,128)(2,1)}, u32[]{:S(2)}, u32[]{:S(2)}) collective-permute-start(bf16[512,512]{1,0:T(8,128)(2,1)} %collective-permute-done.1.refs_3_), channel_id=1, source_target_pairs={{0,8},{8,16},{16,24},{24,32},{32,40},{40,48},{48,56},{56,64},{64,7... | collective-permute-start | bytes 1572872 | tf_op jit(solution)/shard_map/ppermute | solution.py:375
  91.5 12.3 %all-to-all-start.3 = ((f32[8,8,512]{2,1,0:T(8,128)}), f32[8,8,512]{2,1,0:T(8,128)S(1)}, u32[]{:S(2)}, u32[]{:S(2)}) async-start(f32[8,8,512]{2,1,0:T(8,128)} %bitcast.4), calls=%async_computation.3 | async-start | bytes 262144 | tf_op jit(solution)/shard_map/all_to_all | solution.py:278
  96.5 1.0 copy-start.13
  97.5 1.2 copy-start.19
  98.7 5.2 %copy-start.5 = (bf16[512,512]{1,0:T(8,128)(2,1)S(1)}, bf16[512,512]{1,0:T(8,128)(2,1)}, u32[]{:S(2)}) copy-start(bf16[512,512]{1,0:T(8,128)(2,1)} %gate_ref.1) | copy-start | bytes 1572868
  104.6 3.3 %copy-start.14 = (bf16[512,512]{1,0:T(8,128)(2,1)S(1)}, bf16[512,512]{1,0:T(8,128)(2,1)}, u32[]{:S(2)}) copy-start(bf16[512,512]{1,0:T(8,128)(2,1)} %refs_2_.9) | copy-start | bytes 1572868
  104.6 3.3 %copy-start.21 = (f32[4,128,512]{2,1,0:T(8,128)S(1)}, f32[4,128,512]{2,1,0:T(8,128)}, u32[]{:S(2)}) copy-start(f32[4,128,512]{2,1,0:T(8,128)} %copy-done.20) | copy-start | bytes 3145732
  106.0 18.2 %collective-permute-start.3 = (bf16[512,512]{1,0:T(8,128)(2,1)}, bf16[512,512]{1,0:T(8,128)(2,1)S(1)}, u32[]{:S(2)}, u32[]{:S(2)}) collective-permute-start(bf16[512,512]{1,0:T(8,128)(2,1)} %collective-permute-done.2.refs_3_), channel_id=1, source_target_pairs={{0,8},{8,16},{16,24},{24,32},{32,40},{40,48},{48,56},{56,64},{64,7... | collective-permute-start | bytes 1572872 | tf_op jit(solution)/shard_map/ppermute | solution.py:375
  (6 other events, 5.2 us)

commit v4 on v3

--- a/solution.py
+++ b/solution.py
@@ -18,7 +18,7 @@
 LOG_FLOOR = -1000.0
 LOG_ROWS = 16
 SAME = 8
-LINE = 16
+QUAD = 4
 F32 = jnp.float32
 BF16 = jnp.bfloat16
 VMEM_LIMIT = 48 * 1024 * 1024
@@ -28,6 +28,10 @@
 def call(
     body, outs, operands, *, flops, moved, exps=0, scratch=(), smem=(), aliases=None, after=()
 ):
+    count = len(operands)
+    if after:
+        inner = body
+        body = lambda *refs: inner(*refs[:count], *refs[count + len(after) :])
     operands = (*operands, *after)
     spaces = [pltpu.SMEM if i in smem else pltpu.VMEM for i in range(len(operands) - len(after))]
     specs = [pl.BlockSpec(memory_space=m) for m in spaces + [pl.ANY] * len(after)]
@@ -155,11 +159,15 @@
     ]
 
 
-def line_body(got_ref, send_ref):
+def group_body(got_ref, send_ref):
     size = got_ref.shape[1] - LOG_ROWS
     state, total = fold(parts_of(got_ref, size))
-    row = lax.broadcasted_iota(jnp.int32, (send_ref.shape[1] - size, HD), 0)
-    rows = jnp.where(row == 0, total, 0.0)
+    state = state.astype(send_ref.dtype)
+    if send_ref.dtype == F32:
+        row = lax.broadcasted_iota(jnp.int32, (send_ref.shape[1] - size, HD), 0)
+        rows = jnp.where(row == 0, total, 0.0)
+    else:
+        rows = log_rows(total)
     for j in range(send_ref.shape[0]):
         send_ref[j, :size, :] = state
         send_ref[j, size:, :] = rows
@@ -172,10 +180,19 @@
     return state
 
 
-def enter_body(place_ref, line_ref, wide_ref, send_ref):
+def log_before(parts, place):
+    total = jnp.zeros_like(parts[0][1])
+    for j, (_, l) in enumerate(parts[:-1]):
+        total = jnp.where(j < place, total + l, total)
+    return total
+
+
+def enter_body(place_ref, mine_ref, line_ref, wide_ref, send_ref):
     size = send_ref.shape[1]
-    entering = before(parts_of(wide_ref, size), place_ref[0])
-    for j, (s, l) in enumerate(parts_of(line_ref, size)):
+    line = parts_of(line_ref, size)
+    state = before(parts_of(wide_ref, size), place_ref[0])
+    entering = jnp.exp(log_before(line, place_ref[2])) * state + before(line, place_ref[2])
+    for j, (s, l) in enumerate(parts_of(mine_ref, size)):
         send_ref[j] = entering.astype(BF16)
         entering = jnp.exp(l) * entering + s
 
@@ -214,7 +231,7 @@
     send, first, moving = call(
         states_body,
         (
-            jax.ShapeDtypeStruct((LINE, heads * HD // LINE + LOG_ROWS, HD), BF16),
+            jax.ShapeDtypeStruct((QUAD, heads * HD // QUAD + LOG_ROWS, HD), BF16),
             jax.ShapeDtypeStruct((heads, HD, HD), F32),
             jax.ShapeDtypeStruct((tokens, 2 * soft_key.shape[1]), BF16),
         ),
@@ -225,76 +242,33 @@
     return logs, send, first, moving
 
 
-def lightning_local(lin_query, lin_key, lin_value, logs, send, first):
-    tokens, features = lin_query.shape
-    heads = features // HD
-    shards = lax.axis_size("seq")
-    peers = lax.axis_size("head")
-    line = [[LINE * x + z for z in range(LINE)] for x in range(shards // LINE)]
-    wide = [[LINE * x + z for x in range(shards // LINE)] for z in range(LINE)]
-
-    def swap(array, groups):
-        return lax.all_to_all(array, "seq", 0, 0, axis_index_groups=groups, tiled=True)
-
-    lines = swap(send, line)
-    local = call(
-        local_body,
-        jax.ShapeDtypeStruct((tokens, features), F32),
-        (lin_query, lin_key, lin_value, logs, first),
-        flops=4 * tokens * features * BLK,
-        moved=10 * tokens * features,
-    )
-    small = dict(flops=10 * heads * HD * HD, moved=4 * heads * HD * HD)
-    size = heads * HD // LINE
-    total = jax.ShapeDtypeStruct((shards // LINE, size + 8, HD), F32)
-    total = call(line_body, total, (lines,), **small)
-    return local, lines, total, swap, line, wide, small
-
-
-def lightning(lin_query, lin_gate, logs, norm_gain, place, local, lines, total, swap, line, wide, small):
-    tokens, features = lin_query.shape
-    heads = features // HD
-    peers = lax.axis_size("head")
-    size = heads * HD // LINE
-    wides = swap(total, wide)
-    entering = call(
-        enter_body,
-        jax.ShapeDtypeStruct((LINE, size, HD), BF16),
-        (place, lines, wides),
-        smem=(0,),
-        **small,
-    )
-    entering = swap(entering, line).reshape(heads, HD, HD)
-    raw, squares = call(
-        raw_body,
-        (
-            jax.ShapeDtypeStruct((tokens, features), F32),
-            jax.ShapeDtypeStruct((peers * SAME, tokens), F32),
-        ),
-        (lin_query, logs, local, entering),
-        flops=2 * tokens * features * HD,
-        moved=10 * tokens * features,
-    )
-    squares = lax.all_to_all(squares, "head", 0, 0, tiled=True)
-    return call(
-        functools.partial(norm_body, float(features * peers)),
-        jax.ShapeDtypeStruct((tokens, features), BF16),
-        (raw, squares, lin_gate, norm_gain.reshape(1, features)),
-        flops=8 * tokens * features,
-        moved=8 * tokens * features,
-        exps=tokens * features,
-    )
+def swap(array, groups):
+    return lax.all_to_all(array, "seq", 0, 0, axis_index_groups=groups, tiled=True)
+
+
+def gate_body(*refs):
+    pass
+
+
+def gate(array, *after):
+    anywhere = pl.BlockSpec(memory_space=pl.ANY)
+    return pl.pallas_call(
+        gate_body,
+        out_shape=jax.ShapeDtypeStruct(array.shape, array.dtype),
+        in_specs=[anywhere] * (1 + len(after)),
+        out_specs=anywhere,
+        input_output_aliases={0: 0},
+        cost_estimate=pl.CostEstimate(flops=0, bytes_accessed=0, transcendentals=0),
+    )(array, *after)
 
 
 SCALE = math.log2(math.e) * HD ** (-0.5)
 
 
 def attend_body(backs, opening, final, *refs):
-    place_ref, docs_ref, query_ref, piece_ref = refs[:4]
-    pieces = [
-        piece_ref.at[:, 2 * HD * j : 2 * HD * (j + 1)] for j in range(piece_ref.shape[1] // (2 * HD))
-    ]
-    rest = refs[4:]
+    place_ref, docs_ref, query_ref = refs[:3]
+    pieces = refs[3 : 3 + len(backs)]
+    rest = refs[3 + len(backs) :]
     tokens, features = query_ref.shape
     heads = features // HD
     blocks = tokens // MBLK
@@ -364,23 +338,15 @@
                 ].astype(BF16)
 
 
-def join_body(first_ref, second_ref, *rest):
-    both_ref = rest[-1]
-    both_ref[:, : first_ref.shape[1]] = first_ref[...]
-    both_ref[:, first_ref.shape[1] :] = second_ref[...]
-
-
 def forward(array, steps):
     shards = lax.axis_size("seq")
     return lax.ppermute(array, "seq", [(s, s + steps) for s in range(shards - steps)])
 
 
-def attend(soft_query, own, doc_ids, place, after):
+def absorber(soft_query, doc_ids, place):
     tokens, features = soft_query.shape
     blocks = tokens // MBLK
-    hops = (DOC_MOST + blocks - 2) // blocks
     heads = features // HD
-    half = (hops + 1) // 2
     rows = heads * MBLK
     carry = (
         jax.ShapeDtypeStruct((blocks, HD, rows), F32),
@@ -388,8 +354,8 @@
         jax.ShapeDtypeStruct((blocks, 1, rows), F32),
     )
 
-    def absorb(state, backs, array, final=False):
-        operands = (place, doc_ids, soft_query, array, *state)
+    def absorb(state, backs, arrays, final=False):
+        operands = (place, doc_ids, soft_query, *arrays, *state)
         aliases = {len(operands) - 3 + j: j for j in range(3)}
         return call(
             functools.partial(attend_body, backs, not state, final),
@@ -403,21 +369,7 @@
             exps=len(backs) * heads * tokens * tokens,
         )
 
-    far = forward(own, half)
-    state = absorb((), (0,), own)
-    moving = call(
-        join_body,
-        jax.ShapeDtypeStruct((tokens, 2 * own.shape[1]), BF16),
-        (own, far),
-        flops=0,
-        moved=4 * own.size,
-        after=(state[1], *after),
-    )
-    state = absorb(state, (half,), far)
-    for back in range(1, half):
-        moving = forward(moving, 1)
-        state = absorb(state, (back, back + half), moving, back == half - 1)
-    return state
+    return absorb
 
 
 def on_device(
@@ -432,12 +384,95 @@
     soft_value,
     doc_ids,
 ):
+    tokens, features = lin_query.shape
+    heads = features // HD
+    shards = lax.axis_size("seq")
+    peers = lax.axis_size("head")
     shard = lax.axis_index("seq")
-    place = jnp.stack([shard // LINE, shard]).astype(jnp.int32)
-    logs, send, first, moving = states(lin_key, lin_value, log_decay, soft_key, soft_value)
-    parts = lightning_local(lin_query, lin_key, lin_value, logs, send, first)
-    soft_out = attend(soft_query, moving, doc_ids, place, (parts[0], parts[2]))
-    lin_out = lightning(lin_query, lin_gate, logs, norm_gain, place, *parts)
+    span = QUAD * QUAD
+    place = jnp.stack([shard // span, shard, (shard % span) // QUAD]).astype(jnp.int32)
+    near = [[QUAD * g + j for j in range(QUAD)] for g in range(shards // QUAD)]
+    line = [
+        [span * x + QUAD * a + b for a in range(QUAD)]
+        for x in range(shards // span)
+        for b in range(QUAD)
+    ]
+    wide = [[span * x + r for x in range(shards // span)] for r in range(span)]
+    size = heads * HD // QUAD
+    small = dict(flops=10 * heads * HD * HD, moved=4 * heads * HD * HD)
+    hops = (DOC_MOST + tokens // MBLK - 2) // (tokens // MBLK)
+    absorb = absorber(soft_query, doc_ids, place)
+
+    logs, send, first, own = states(lin_key, lin_value, log_decay, soft_key, soft_value)
+    mine = swap(send, near)
+    back = [own]
+
+    def hop(*after):
+        if after:
+            back[-1] = gate(back[-1], *after)
+        back.append(forward(back[-1], 1))
+
+    hop()
+    local = call(
+        local_body,
+        jax.ShapeDtypeStruct((tokens, features), F32),
+        (lin_query, lin_key, lin_value, logs, first),
+        flops=4 * tokens * features * BLK,
+        moved=10 * tokens * features,
+    )
+    state = absorb((), (0,), back[:1])
+    hop(local, state[1])
+    group = call(
+        group_body,
+        jax.ShapeDtypeStruct((QUAD, size + LOG_ROWS, HD), BF16),
+        (mine,),
+        **small,
+    )
+    lines = swap(group, line)
+    hop(group)
+    state = absorb(state, (1, 2), back[1:3])
+    hop(state[1])
+    total = call(
+        group_body,
+        jax.ShapeDtypeStruct((shards // span, size + 8, HD), F32),
+        (lines,),
+        **small,
+    )
+    wides = swap(total, wide)
+    hop(total)
+    state = absorb(state, (3, 4), back[3:5])
+    hop(state[1])
+    entering = call(
+        enter_body,
+        jax.ShapeDtypeStruct((QUAD, size, HD), BF16),
+        (place, mine, lines, wides),
+        smem=(0,),
+        **small,
+    )
+    hop(entering)
+    entering = swap(entering, near).reshape(heads, HD, HD)
+    state = absorb(state, (5, 6), back[5:7])
+    raw, squares = call(
+        raw_body,
+        (
+            jax.ShapeDtypeStruct((tokens, features), F32),
+            jax.ShapeDtypeStruct((peers * SAME, tokens), F32),
+        ),
+        (lin_query, logs, local, entering),
+        flops=2 * tokens * features * HD,
+        moved=10 * tokens * features,
+    )
+    squares = lax.all_to_all(squares, "head", 0, 0, tiled=True)
+    lin_out = call(
+        functools.partial(norm_body, float(features * peers)),
+        jax.ShapeDtypeStruct((tokens, features), BF16),
+        (raw, squares, lin_gate, norm_gain.reshape(1, features)),
+        flops=8 * tokens * features,
+        moved=8 * tokens * features,
+        exps=tokens * features,
+    )
+    assert len(back) == hops + 1
+    soft_out = absorb(state, tuple(range(7, hops + 1)), back[7:], True)
     return (lin_out, soft_out)
 
 

time: 130 us -> 120 us (0.923)
  the two profiles are of different devices: /device:TPU:10 before, /device:TPU:22 now
where the time goes in v4:
time: 120 us; the launch traced here: 118 us
  starting transfers between devices  41.7 us (35%)
  Pallas kernels  31.7 us (26%)
  waiting for transfers between devices  23.1 us (19%)
  local copies, waits for them, and re-layouts  20.7 us (17%)
    pallas_call x12, Pallas kernels, call(): pl.pallas_call(body, out_shape=outs, in_specs=specs, out_specs=jax.tree.m...  31.7 us
    ppermute x7, waiting for transfers between devices, forward(): lax.ppermute(array, 'seq', [(s, s + steps) for s in range(shards - steps)])  23.1 us
    all_to_all x4, starting transfers between devices, swap(): lax.all_to_all(array, 'seq', 0, 0, axis_index_groups=groups, tiled=True)  21 us
    unnamed x86, local copies, waits for them, and re-layouts  20.7 us
    ppermute x7, starting transfers between devices, forward(): lax.ppermute(array, 'seq', [(s, s + steps) for s in range(shards - steps)])  15.7 us
    all_to_all x1, starting transfers between devices, on_device(): squares = lax.all_to_all(squares, 'head', 0, 0, tiled=True)  4.93 us
  transfers between devices with their start and end apart: 12, of which 5 were waited for; matrix products, arithmetic and copies ran while one was open for 0% of the time, Pallas kernels for 22%

profile of v4, /device:TPU:22, one launch (start us, length us, event | category | flops | bytes accessed | tf_op | source)
XLA Modules:
  0.0 118.4 jit_solution(12681035551248456417)
XLA Ops:
  5.2 2.1 %shard_map.113 = (bf16[4,144,128]{2,1,0:T(8,128)(2,1)}, f32[4,128,128]{2,1,0:T(8,128)S(1)}, bf16[512,256]{1,0:T(8,128)(2,1)S(1)}) custom-call(bf16[512,512]{1,0:T(8,128)(2,1)S(1)} %copy-done.2, bf16[512,512]{1,0:T(8,128)(2,1)S(1)} %copy-done.4, f32[4,512]{1,0:T(4,128)S(1)} %bitcast.8, bf16[512,128]{1,0:T(8,128)(2,1)S(1)} %copy-done.20, ...), custom_call_target="tpu_custom_call" | custom-call | flops 134217728 | bytes 1048576 | tf_op jit(solution)/shard_map/pallas_call | solution.py:38
  7.4 5.9 %all-to-all-start = ((bf16[4,144,128]{2,1,0:T(8,128)(2,1)}), bf16[4,144,128]{2,1,0:T(8,128)(2,1)S(1)}, u32[]{:S(2)}, u32[]{:S(2)}) async-start(bf16[4,144,128]{2,1,0:T(8,128)(2,1)} %get-tuple-element.20), calls=%async_computation | async-start | bytes 294912 | tf_op jit(solution)/shard_map/all_to_all | solution.py:246
  13.3 3.9 %collective-permute-start = (bf16[512,256]{1,0:T(8,128)(2,1)S(1)}, bf16[512,256]{1,0:T(8,128)(2,1)S(1)}, u32[]{:S(2)}, u32[]{:S(2)}) collective-permute-start(bf16[512,256]{1,0:T(8,128)(2,1)S(1)} %get-tuple-element.23.refs_3_), channel_id=1, source_target_pairs={{0,8},{8,16},{16,24},{24,32},{32,40},{40,48},{48,56},{56,64},{64,7... | collective-permute-start | bytes 786440 | tf_op jit(solution)/shard_map/ppermute | solution.py:343
  17.9 2.4 %shard_map.120 = (f32[4,128,512]{2,1,0:T(8,128)S(1)}, f32[4,1,512]{2,1,0:T(1,128)S(1)}, f32[4,1,512]{2,1,0:T(1,128)S(1)}) custom-call(s32[3]{0:T(128)S(1)} %pad_add_fusion.place_ref.refs_0_, s32[256]{0:T(256)S(1)} %copy-done.34, bf16[512,512]{1,0:T(8,128)(2,1)S(1)} %copy-done.31, bf16[512,256]{1,0:T(8,128)(2,1)S(1)} %get-tuple-element.23.refs_3_), custom_call_target="tpu_custom_call" | custom-call | flops 4000000000 | bytes 3145728 | tf_op jit(solution)/shard_map/pallas_call | solution.py:38
  20.3 2.0 %shard_map.114.local_ref.refs_1_ = f32[512,512]{1,0:T(8,128)S(1)} custom-call(bf16[512,512]{1,0:T(8,128)(2,1)S(1)} %copy-done.6, bf16[512,512]{1,0:T(8,128)(2,1)S(1)} %copy-done.3, bf16[512,512]{1,0:T(8,128)(2,1)S(1)} %copy-done.5, f32[4,512]{1,0:T(4,128)S(1)} %bitcast.9, f32[4,128,128]{2,1,0:T(8,128)S(1)} %get-tuple-element.19.first_ref), custom_call_target="tpu_custom_call" | custom-call | flops 268435456 | bytes 2621440 | tf_op jit(solution)/shard_map/pallas_call | solution.py:38
  23.4 6.9 %collective-permute-done.refs_0_ = bf16[512,256]{1,0:T(8,128)(2,1)S(1)} collective-permute-done((bf16[512,256]{1,0:T(8,128)(2,1)S(1)}, bf16[512,256]{1,0:T(8,128)(2,1)S(1)}, u32[]{:S(2)}, u32[]{:S(2)}) %collective-permute-start) | collective-permute-done | bytes 262176 | tf_op jit(solution)/shard_map/ppermute | solution.py:343
  30.9 2.0 %collective-permute-start.1 = (bf16[512,256]{1,0:T(8,128)(2,1)}, bf16[512,256]{1,0:T(8,128)(2,1)S(1)}, u32[]{:S(2)}, u32[]{:S(2)}) collective-permute-start(bf16[512,256]{1,0:T(8,128)(2,1)} %shard_map.121.refs_3_), channel_id=1, source_target_pairs={{0,8},{8,16},{16,24},{24,32},{32,40},{40,48},{48,56},{56,64},{64,7... | collective-permute-start | bytes 786440 | tf_op jit(solution)/shard_map/ppermute | solution.py:343
  33.7 7.2 %all-to-all-start.1 = ((bf16[4,144,128]{2,1,0:T(8,128)(2,1)}), bf16[4,144,128]{2,1,0:T(8,128)(2,1)S(1)}, u32[]{:S(2)}, u32[]{:S(2)}) async-start(bf16[4,144,128]{2,1,0:T(8,128)(2,1)} %shard_map.115.refs_1_), calls=%async_computation.1 | async-start | bytes 294912 | tf_op jit(solution)/shard_map/all_to_all | solution.py:246
  43.1 2.1 %collective-permute-start.2 = (bf16[512,256]{1,0:T(8,128)(2,1)}, bf16[512,256]{1,0:T(8,128)(2,1)S(1)}, u32[]{:S(2)}, u32[]{:S(2)}) collective-permute-start(bf16[512,256]{1,0:T(8,128)(2,1)} %shard_map.122.refs_4_), channel_id=1, source_target_pairs={{0,8},{8,16},{16,24},{24,32},{32,40},{40,48},{48,56},{56,64},{64,7... | collective-permute-start | bytes 786440 | tf_op jit(solution)/shard_map/ppermute | solution.py:343
  46.3 5.0 %shard_map.123 = (f32[4,128,512]{2,1,0:T(8,128)S(1)}, f32[4,1,512]{2,1,0:T(1,128)S(1)}, f32[4,1,512]{2,1,0:T(1,128)S(1)}) custom-call(s32[3]{0:T(128)S(1)} %pad_add_fusion.place_ref.refs_0_, s32[256]{0:T(256)S(1)} %copy-done.34, bf16[512,512]{1,0:T(8,128)(2,1)S(1)} %copy-done.31, ...), custom_call_target="tpu_custom_call", output_to_operand_aliasing={{0}: (5, {}), {1}: (6, {}), {2}: (7, {})} | custom-call | flops 8000000000 | bytes 3145728 | tf_op jit(solution)/shard_map/pallas_call | solution.py:38
  52.8 5.6 %collective-permute-done.2.refs_0_ = bf16[512,256]{1,0:T(8,128)(2,1)S(1)} collective-permute-done((bf16[512,256]{1,0:T(8,128)(2,1)}, bf16[512,256]{1,0:T(8,128)(2,1)S(1)}, u32[]{:S(2)}, u32[]{:S(2)}) %collective-permute-start.2) | collective-permute-done | bytes 262176 | tf_op jit(solution)/shard_map/ppermute | solution.py:343
  59.1 1.9 %collective-permute-start.3 = (bf16[512,256]{1,0:T(8,128)(2,1)}, bf16[512,256]{1,0:T(8,128)(2,1)S(1)}, u32[]{:S(2)}, u32[]{:S(2)}) collective-permute-start(bf16[512,256]{1,0:T(8,128)(2,1)} %shard_map.124.refs_3_), channel_id=1, source_target_pairs={{0,8},{8,16},{16,24},{24,32},{32,40},{40,48},{48,56},{56,64},{64,7... | collective-permute-start | bytes 786440 | tf_op jit(solution)/shard_map/ppermute | solution.py:343
  61.8 4.5 %all-to-all-start.2 = ((f32[4,136,128]{2,1,0:T(8,128)}), f32[4,136,128]{2,1,0:T(8,128)S(1)}, u32[]{:S(2)}, u32[]{:S(2)}) async-start(f32[4,136,128]{2,1,0:T(8,128)} %shard_map.116.refs_1_), calls=%async_computation.2 | async-start | bytes 557056 | tf_op jit(solution)/shard_map/all_to_all | solution.py:246
  66.3 4.8 %collective-permute-done.3.refs_0_ = bf16[512,256]{1,0:T(8,128)(2,1)S(1)} collective-permute-done((bf16[512,256]{1,0:T(8,128)(2,1)}, bf16[512,256]{1,0:T(8,128)(2,1)S(1)}, u32[]{:S(2)}, u32[]{:S(2)}) %collective-permute-start.3) | collective-permute-done | bytes 262176 | tf_op jit(solution)/shard_map/ppermute | solution.py:343
  71.8 1.9 %collective-permute-start.4 = (bf16[512,256]{1,0:T(8,128)(2,1)}, bf16[512,256]{1,0:T(8,128)(2,1)S(1)}, u32[]{:S(2)}, u32[]{:S(2)}) collective-permute-start(bf16[512,256]{1,0:T(8,128)(2,1)} %shard_map.125.refs_4_), channel_id=1, source_target_pairs={{0,8},{8,16},{16,24},{24,32},{32,40},{40,48},{48,56},{56,64},{64,7... | collective-permute-start | bytes 786440 | tf_op jit(solution)/shard_map/ppermute | solution.py:343
  75.0 3.5 %all-to-all-start.3 = ((bf16[4,128,128]{2,1,0:T(8,128)(2,1)}), bf16[4,128,128]{2,1,0:T(8,128)(2,1)S(1)}, u32[]{:S(2)}, u32[]{:S(2)}) async-start(bf16[4,128,128]{2,1,0:T(8,128)(2,1)} %shard_map.117.refs_1_), calls=%async_computation.3 | async-start | bytes 262144 | tf_op jit(solution)/shard_map/all_to_all | solution.py:246
  80.8 4.8 %shard_map.126 = (f32[4,128,512]{2,1,0:T(8,128)S(1)}, f32[4,1,512]{2,1,0:T(1,128)S(1)}, f32[4,1,512]{2,1,0:T(1,128)S(1)}) custom-call(s32[3]{0:T(128)S(1)} %pad_add_fusion.place_ref.refs_0_, s32[256]{0:T(256)S(1)} %copy-done.34, bf16[512,512]{1,0:T(8,128)(2,1)S(1)} %copy-done.32, ...), custom_call_target="tpu_custom_call", output_to_operand_aliasing={{0}: (5, {}), {1}: (6, {}), {2}: (7, {})} | custom-call | flops 8000000000 | bytes 3145728 | tf_op jit(solution)/shard_map/pallas_call | solution.py:38
  87.9 1.9 %collective-permute-start.5 = (bf16[512,256]{1,0:T(8,128)(2,1)}, bf16[512,256]{1,0:T(8,128)(2,1)S(1)}, u32[]{:S(2)}, u32[]{:S(2)}) collective-permute-start(bf16[512,256]{1,0:T(8,128)(2,1)} %shard_map.127.refs_3_), channel_id=1, source_target_pairs={{0,8},{8,16},{16,24},{24,32},{32,40},{40,48},{48,56},{56,64},{64,7... | collective-permute-start | bytes 786440 | tf_op jit(solution)/shard_map/ppermute | solution.py:343
  89.8 2.5 %shard_map.118 = (f32[512,512]{1,0:T(8,128)S(1)}, f32[64,512]{1,0:T(8,128)}) custom-call(bf16[512,512]{1,0:T(8,128)(2,1)S(1)} %copy-done.6, f32[4,512]{1,0:T(4,128)S(1)} %bitcast.10, f32[512,512]{1,0:T(8,128)S(1)} %copy-done.1, bf16[4,128,128]{2,1,0:T(8,128)(2,1)S(1)} %all-to-all-done.3.enter_ref), custom_call_target="tpu_custom_call" | custom-call | flops 67108864 | bytes 2621440 | tf_op jit(solution)/shard_map/pallas_call | solution.py:38
  92.3 4.9 %all-to-all-start.4 = ((f32[8,8,512]{2,1,0:T(8,128)}), f32[8,8,512]{2,1,0:T(8,128)S(1)}, u32[]{:S(2)}, u32[]{:S(2)}) async-start(f32[8,8,512]{2,1,0:T(8,128)} %bitcast.4), calls=%async_computation.4 | async-start | bytes 262144 | tf_op jit(solution)/shard_map/all_to_all | solution.py:465
  97.2 4.3 %collective-permute-done.5.refs_0_ = bf16[512,256]{1,0:T(8,128)(2,1)S(1)} collective-permute-done((bf16[512,256]{1,0:T(8,128)(2,1)}, bf16[512,256]{1,0:T(8,128)(2,1)S(1)}, u32[]{:S(2)}, u32[]{:S(2)}) %collective-permute-start.5) | collective-permute-done | bytes 262176 | tf_op jit(solution)/shard_map/ppermute | solution.py:343
  102.2 1.9 %collective-permute-start.6 = (bf16[512,256]{1,0:T(8,128)(2,1)}, bf16[512,256]{1,0:T(8,128)(2,1)S(1)}, u32[]{:S(2)}, u32[]{:S(2)}) collective-permute-start(bf16[512,256]{1,0:T(8,128)(2,1)} %shard_map.128.refs_4_), channel_id=1, source_target_pairs={{0,8},{8,16},{16,24},{24,32},{32,40},{40,48},{48,56},{56,64},{64,7... | collective-permute-start | bytes 786440 | tf_op jit(solution)/shard_map/ppermute | solution.py:343
  106.4 5.0 %shard_map.129 = (f32[4,128,512]{2,1,0:T(8,128)S(1)}, f32[4,1,512]{2,1,0:T(1,128)S(1)}, f32[4,1,512]{2,1,0:T(1,128)S(1)}) custom-call(s32[3]{0:T(128)S(1)} %pad_add_fusion.place_ref.refs_0_, s32[256]{0:T(256)S(1)} %copy-done.34, bf16[512,512]{1,0:T(8,128)(2,1)S(1)} %copy-done.33, ...), custom_call_target="tpu_custom_call", output_to_operand_aliasing={{0}: (5, {}), {1}: (6, {}), {2}: (7, {})} | custom-call | flops 8000000000 | bytes 3145728 | tf_op jit(solution)/shard_map/pallas_call | solution.py:38
  114.5 3.9 %shard_map.130 = bf16[512,512]{1,0:T(8,128)(2,1)} custom-call(s32[3]{0:T(128)S(1)} %pad_add_fusion.place_ref.refs_0_, s32[256]{0:T(256)S(1)} %copy-done.34, bf16[512,512]{1,0:T(8,128)(2,1)S(1)} %copy-done.33, bf16[512,256]{1,0:T(8,128)(2,1)S(1)} %collective-permute-done.6.refs_3_, f32[4,128,512]{2,1,0:T(8,128)S(1)} %copy-done.42, ...), custom_call_target="tpu_custom_call" | custom-call | flops 4000000000 | bytes 3145728 | tf_op jit(solution)/shard_map/pallas_call | solution.py:38
  (105 shorter events, 26.6 us)
Async XLA Ops:
  5.2 12.1 %copy-start.31 = (bf16[512,512]{1,0:T(8,128)(2,1)S(1)}, bf16[512,512]{1,0:T(8,128)(2,1)}, u32[]{:S(2)}) copy-start(bf16[512,512]{1,0:T(8,128)(2,1)} %refs_2_.9) | copy-start | bytes 1572868
  7.4 25.6 %all-to-all-start = ((bf16[4,144,128]{2,1,0:T(8,128)(2,1)}), bf16[4,144,128]{2,1,0:T(8,128)(2,1)S(1)}, u32[]{:S(2)}, u32[]{:S(2)}) async-start(bf16[4,144,128]{2,1,0:T(8,128)(2,1)} %get-tuple-element.20), calls=%async_computation | async-start | bytes 294912 | tf_op jit(solution)/shard_map/all_to_all | solution.py:246
  13.3 17.0 %collective-permute-start = (bf16[512,256]{1,0:T(8,128)(2,1)S(1)}, bf16[512,256]{1,0:T(8,128)(2,1)S(1)}, u32[]{:S(2)}, u32[]{:S(2)}) collective-permute-start(bf16[512,256]{1,0:T(8,128)(2,1)S(1)} %get-tuple-element.23.refs_3_), channel_id=1, source_target_pairs={{0,8},{8,16},{16,24},{24,32},{32,40},{40,48},{48,56},{56,64},{64,7... | collective-permute-start | bytes 786440 | tf_op jit(solution)/shard_map/ppermute | solution.py:343
  30.9 14.3 %copy-start.36 = (f32[4,128,512]{2,1,0:T(8,128)S(1)}, f32[4,128,512]{2,1,0:T(8,128)}, u32[]{:S(2)}) copy-start(f32[4,128,512]{2,1,0:T(8,128)} %copy-done.35) | copy-start | bytes 3145732
  30.9 11.5 %collective-permute-start.1 = (bf16[512,256]{1,0:T(8,128)(2,1)}, bf16[512,256]{1,0:T(8,128)(2,1)S(1)}, u32[]{:S(2)}, u32[]{:S(2)}) collective-permute-start(bf16[512,256]{1,0:T(8,128)(2,1)} %shard_map.121.refs_3_), channel_id=1, source_target_pairs={{0,8},{8,16},{16,24},{24,32},{32,40},{40,48},{48,56},{56,64},{64,7... | collective-permute-start | bytes 786440 | tf_op jit(solution)/shard_map/ppermute | solution.py:343
  33.7 27.3 %all-to-all-start.1 = ((bf16[4,144,128]{2,1,0:T(8,128)(2,1)}), bf16[4,144,128]{2,1,0:T(8,128)(2,1)S(1)}, u32[]{:S(2)}, u32[]{:S(2)}) async-start(bf16[4,144,128]{2,1,0:T(8,128)(2,1)} %shard_map.115.refs_1_), calls=%async_computation.1 | async-start | bytes 294912 | tf_op jit(solution)/shard_map/all_to_all | solution.py:246
  40.9 4.4 %copy-start.17 = (bf16[512,256]{1,0:T(8,128)(2,1)S(1)}, bf16[512,256]{1,0:T(8,128)(2,1)}, u32[]{:S(2)}) copy-start(bf16[512,256]{1,0:T(8,128)(2,1)} %shard_map.121.refs_3_) | copy-start | bytes 786436
  40.9 4.4 %copy-start.25 = (f32[4,1,512]{2,1,0:T(1,128)S(1)}, f32[4,1,512]{2,1,0:T(1,128)}, u32[]{:S(2)}) copy-start(f32[4,1,512]{2,1,0:T(1,128)} %copy-done.24) | copy-start | bytes 24580
  43.1 15.2 %collective-permute-start.2 = (bf16[512,256]{1,0:T(8,128)(2,1)}, bf16[512,256]{1,0:T(8,128)(2,1)S(1)}, u32[]{:S(2)}, u32[]{:S(2)}) collective-permute-start(bf16[512,256]{1,0:T(8,128)(2,1)} %shard_map.122.refs_4_), channel_id=1, source_target_pairs={{0,8},{8,16},{16,24},{24,32},{32,40},{40,48},{48,56},{56,64},{64,7... | collective-permute-start | bytes 786440 | tf_op jit(solution)/shard_map/ppermute | solution.py:343
  59.1 12.0 %collective-permute-start.3 = (bf16[512,256]{1,0:T(8,128)(2,1)}, bf16[512,256]{1,0:T(8,128)(2,1)S(1)}, u32[]{:S(2)}, u32[]{:S(2)}) collective-permute-start(bf16[512,256]{1,0:T(8,128)(2,1)} %shard_map.124.refs_3_), channel_id=1, source_target_pairs={{0,8},{8,16},{16,24},{24,32},{32,40},{40,48},{48,56},{56,64},{64,7... | collective-permute-start | bytes 786440 | tf_op jit(solution)/shard_map/ppermute | solution.py:343
  61.8 11.9 %all-to-all-start.2 = ((f32[4,136,128]{2,1,0:T(8,128)}), f32[4,136,128]{2,1,0:T(8,128)S(1)}, u32[]{:S(2)}, u32[]{:S(2)}) async-start(f32[4,136,128]{2,1,0:T(8,128)} %shard_map.116.refs_1_), calls=%async_computation.2 | async-start | bytes 557056 | tf_op jit(solution)/shard_map/all_to_all | solution.py:246
  71.8 15.4 %collective-permute-start.4 = (bf16[512,256]{1,0:T(8,128)(2,1)}, bf16[512,256]{1,0:T(8,128)(2,1)S(1)}, u32[]{:S(2)}, u32[]{:S(2)}) collective-permute-start(bf16[512,256]{1,0:T(8,128)(2,1)} %shard_map.125.refs_4_), channel_id=1, source_target_pairs={{0,8},{8,16},{16,24},{24,32},{32,40},{40,48},{48,56},{56,64},{64,7... | collective-permute-start | bytes 786440 | tf_op jit(solution)/shard_map/ppermute | solution.py:343
  73.7 4.8 %copy-start.15 = (bf16[512,256]{1,0:T(8,128)(2,1)S(1)}, bf16[512,256]{1,0:T(8,128)(2,1)}, u32[]{:S(2)}) copy-start(bf16[512,256]{1,0:T(8,128)(2,1)} %shard_map.124.refs_3_) | copy-start | bytes 786436
  73.7 4.8 %copy-start.27 = (f32[4,1,512]{2,1,0:T(1,128)S(1)}, f32[4,1,512]{2,1,0:T(1,128)}, u32[]{:S(2)}) copy-start(f32[4,1,512]{2,1,0:T(1,128)} %copy-done.26) | copy-start | bytes 24580
  75.0 3.5 %copy-start.9 = (bf16[512,256]{1,0:T(8,128)(2,1)S(1)}, bf16[512,256]{1,0:T(8,128)(2,1)}, u32[]{:S(2)}) copy-start(bf16[512,256]{1,0:T(8,128)(2,1)} %shard_map.125.refs_4_) | copy-start | bytes 786436
  75.0 14.8 %all-to-all-start.3 = ((bf16[4,128,128]{2,1,0:T(8,128)(2,1)}), bf16[4,128,128]{2,1,0:T(8,128)(2,1)S(1)}, u32[]{:S(2)}, u32[]{:S(2)}) async-start(bf16[4,128,128]{2,1,0:T(8,128)(2,1)} %shard_map.117.refs_1_), calls=%async_computation.3 | async-start | bytes 262144 | tf_op jit(solution)/shard_map/all_to_all | solution.py:246
  80.8 9.0 %copy-start.1 = (f32[512,512]{1,0:T(8,128)S(1)}, f32[512,512]{1,0:T(8,128)}, u32[]{:S(2)}) copy-start(f32[512,512]{1,0:T(8,128)} %copy-done) | copy-start | bytes 3145732
  87.9 13.7 %collective-permute-start.5 = (bf16[512,256]{1,0:T(8,128)(2,1)}, bf16[512,256]{1,0:T(8,128)(2,1)S(1)}, u32[]{:S(2)}, u32[]{:S(2)}) collective-permute-start(bf16[512,256]{1,0:T(8,128)(2,1)} %shard_map.127.refs_3_), channel_id=1, source_target_pairs={{0,8},{8,16},{16,24},{24,32},{32,40},{40,48},{48,56},{56,64},{64,7... | collective-permute-start | bytes 786440 | tf_op jit(solution)/shard_map/ppermute | solution.py:343
  92.3 11.9 %copy-start.33 = (bf16[512,512]{1,0:T(8,128)(2,1)S(1)}, bf16[512,512]{1,0:T(8,128)(2,1)}, u32[]{:S(2)}) copy-start(bf16[512,512]{1,0:T(8,128)(2,1)} %refs_2_.9) | copy-start | bytes 1572868
  92.3 20.1 %all-to-all-start.4 = ((f32[8,8,512]{2,1,0:T(8,128)}), f32[8,8,512]{2,1,0:T(8,128)S(1)}, u32[]{:S(2)}, u32[]{:S(2)}) async-start(f32[8,8,512]{2,1,0:T(8,128)} %bitcast.4), calls=%async_computation.4 | async-start | bytes 262144 | tf_op jit(solution)/shard_map/all_to_all | solution.py:465
  97.2 7.0 %copy-start.11 = (bf16[512,256]{1,0:T(8,128)(2,1)S(1)}, bf16[512,256]{1,0:T(8,128)(2,1)}, u32[]{:S(2)}) copy-start(bf16[512,256]{1,0:T(8,128)(2,1)} %shard_map.127.refs_3_) | copy-start | bytes 786436
  97.2 7.0 %copy-start.29 = (f32[4,1,512]{2,1,0:T(1,128)S(1)}, f32[4,1,512]{2,1,0:T(1,128)}, u32[]{:S(2)}) copy-start(f32[4,1,512]{2,1,0:T(1,128)} %copy-done.28) | copy-start | bytes 24580
  102.2 12.2 %collective-permute-start.6 = (bf16[512,256]{1,0:T(8,128)(2,1)}, bf16[512,256]{1,0:T(8,128)(2,1)S(1)}, u32[]{:S(2)}, u32[]{:S(2)}) collective-permute-start(bf16[512,256]{1,0:T(8,128)(2,1)} %shard_map.128.refs_4_), channel_id=1, source_target_pairs={{0,8},{8,16},{16,24},{24,32},{32,40},{40,48},{48,56},{56,64},{64,7... | collective-permute-start | bytes 786440 | tf_op jit(solution)/shard_map/ppermute | solution.py:343
  106.4 6.0 %copy-start.7 = (bf16[512,512]{1,0:T(8,128)(2,1)S(1)}, bf16[512,512]{1,0:T(8,128)(2,1)}, u32[]{:S(2)}) copy-start(bf16[512,512]{1,0:T(8,128)(2,1)} %gate_ref.1) | copy-start | bytes 1572868
  (31 other events, 36.0 us)
